TPU v7x, 32 devices: a whole 2x2x4 slice. The times are simulated.
32 devices in a mesh: pipe: 2 (over core), seq: 4 (over z), dp: 4 (over y, x).
Axes of the slice: x: 2, y: 2, z: 4, core: 2. Of those that a mesh axis runs over, the one named last changes fastest.
Arguments:
- images: bfloat16 [8, 1376, 1024], P('dp', 'seq'), may hold values from -6 to 6
- key_mask: int32 [8, 1376], P('dp', 'seq'), may hold values from 0 to 1, as said below
- w_qkv: bfloat16 [2, 1024, 3072], P('pipe', 'dp'), may hold values from -0.1875 to 0.1875
- w_proj: bfloat16 [2, 1024, 1024], P('pipe', 'dp'), may hold values from -0.375 to 0.375
- w_fc1: bfloat16 [2, 1024, 4096], P('pipe', 'dp'), may hold values from -0.1875 to 0.1875
- w_fc2: bfloat16 [2, 4096, 1024], P('pipe', 'dp'), may hold values from -0.09375 to 0.09375
- gains: float32 [2, 4, 1024], P('pipe', None, 'dp'), may hold values from 0.1 to 1.9
- biases: float32 [2, 6, 1024], P('pipe', None, 'dp'), may hold values from -1.8 to 1.8
- fc1_bias: float32 [2, 4096], P('pipe', 'dp'), may hold values from -1.8 to 1.8
- out_grad: bfloat16 [8, 1376, 1024], P('dp', 'seq'), may hold values from -6 to 6
Outputs:
- section_outputs: bfloat16 [2, 8, 1376, 1024], P('pipe', 'dp', 'seq')
- input_grads: bfloat16 [2, 8, 1376, 1024], P('pipe', 'dp', 'seq')
- grad_qkv: float32 [2, 1024, 3072], P('pipe', ('seq', 'dp'))
- grad_proj: float32 [2, 1024, 1024], P('pipe', ('seq', 'dp'))
- grad_fc1: float32 [2, 1024, 4096], P('pipe', ('seq', 'dp'))
- grad_fc2: float32 [2, 4096, 1024], P('pipe', ('seq', 'dp'))
- grad_gains: float32 [2, 4, 1024], P('pipe', None, ('seq', 'dp'))
- grad_biases: float32 [2, 6, 1024], P('pipe', None, ('seq', 'dp'))
- grad_fc1_bias: float32 [2, 4096], P('pipe', ('seq', 'dp'))
Inputs may be any that keep to these rules, and one draw needn't show every extreme that they name: In every image the ones of key_mask are a prefix of its tokens, 688 tokens long or longer.
All inputs are finite; a program needn't handle non-finite values.
Results may differ from a plain program's by a relative error of at most 0.03.
Values may be sent and summed in bfloat16 or wider, within the bound.
A program may use at most 256 MiB of HBM per device.

v0:
```python
import jax
import jax.numpy as jnp
from jax import lax
from jax.sharding import PartitionSpec as P

D = 1024
H = 16
HD = 64
MICRO = 2


epsilon = 1e-06
root_half = 0.7071067811865476
inv_root_tau = 0.3989422804014327


def shifted_2(block, axis, distance):
    devices = range(lax.axis_size(axis))
    route = [(i - distance, i) for i in devices if i - distance in devices]
    return lax.ppermute(block, axis, route)


def layer_norm(values):
    centre = jnp.mean(values, axis=-1, keepdims=True)
    shifted = values - centre
    factor = lax.rsqrt(jnp.mean(shifted * shifted, axis=-1, keepdims=True) + epsilon)
    return (shifted * factor, factor)


def norm_back(upward, normed, factor):
    inner = (
        upward
        - jnp.mean(upward, axis=-1, keepdims=True)
        - normed * jnp.mean(upward * normed, axis=-1, keepdims=True)
    )
    return factor * inner


def gelu_value(hidden):
    return 0.5 * hidden * (1.0 + lax.erf(hidden * root_half))


def gelu_slope(hidden):
    return (
        0.5 * (1.0 + lax.erf(hidden * root_half))
        + hidden * jnp.exp(-0.5 * hidden * hidden) * inv_root_tau
    )


def masked_scores(queries, key_rows, visible):
    scores = jnp.dot(queries, key_rows.T, preferred_element_type=jnp.float32) * 0.125
    return jnp.where(visible[None, :], scores, -1e30)


def head_forward(pieces):
    queries, key_rows, values, visible = pieces
    scores = masked_scores(queries, key_rows, visible)
    highest = jnp.max(scores, axis=-1, keepdims=True)
    weights = jnp.exp(scores - highest)
    totals = jnp.sum(weights, axis=-1, keepdims=True)
    attention = (weights / totals).astype(jnp.bfloat16)
    result = jnp.dot(attention, values, preferred_element_type=jnp.float32)
    return (result.astype(jnp.bfloat16), (highest + jnp.log(totals))[:, 0])


def head_backward(pieces):
    queries, key_rows, values, visible, log_total, upward = pieces
    scores = masked_scores(queries, key_rows, visible)
    attention = jnp.exp(scores - log_total[:, None])
    slopes = jnp.dot(upward, values.T, preferred_element_type=jnp.float32)
    centred = slopes - jnp.sum(attention * slopes, axis=-1, keepdims=True)
    score_grads = (attention * centred).astype(jnp.bfloat16)
    grad_query = jnp.dot(score_grads, key_rows, preferred_element_type=jnp.float32) * 0.125
    grad_keys = jnp.dot(score_grads.T, queries, preferred_element_type=jnp.float32) * 0.125
    grad_values = jnp.dot(
        attention.astype(jnp.bfloat16).T, upward, preferred_element_type=jnp.float32
    )
    return jnp.stack([grad_query, grad_keys, grad_values]).astype(jnp.bfloat16)


def forward_layer(section_in, visible, weight_set):
    w_qkv, w_proj, w_fc1, w_fc2, gains, biases, fc1_bias = weight_set
    seq_count = lax.axis_size("seq")
    group_heads = H // seq_count
    group_width = D // seq_count
    image_count = section_in.shape[0]
    local_rows = section_in.shape[1]
    full_rows = local_rows * seq_count
    frames = section_in.astype(jnp.float32)
    normed_one, factor_one = layer_norm(frames)
    normed_in = (normed_one * gains[0] + biases[0]).astype(jnp.bfloat16)
    projected = jnp.einsum("bnd,de->bne", normed_in, w_qkv, preferred_element_type=jnp.float32)
    bias_row = jnp.concatenate([biases[1], jnp.zeros_like(biases[1]), biases[2]])
    packed = (projected + bias_row).astype(jnp.bfloat16)
    spread = lax.all_to_all(
        packed.reshape(image_count, local_rows, 3, seq_count, group_width),
        "seq",
        split_axis=3,
        concat_axis=1,
        tiled=True,
    )
    head_sets = (
        spread.reshape(image_count, full_rows, 3, group_heads, HD)
        .transpose(2, 0, 3, 1, 4)
        .reshape(3, image_count * group_heads, full_rows, HD)
    )
    visible_rows = jnp.repeat(visible, group_heads, axis=0)
    head_outs, log_total = lax.map(
        head_forward, (head_sets[0], head_sets[1], head_sets[2], visible_rows)
    )
    merged = (
        head_outs.reshape(image_count, group_heads, full_rows, HD)
        .transpose(0, 2, 1, 3)
        .reshape(image_count, full_rows, group_width)
    )
    token_outs = lax.all_to_all(merged, "seq", split_axis=1, concat_axis=2, tiled=True)
    branch_one = (
        jnp.einsum("bnd,de->bne", token_outs, w_proj, preferred_element_type=jnp.float32)
        + biases[3]
    )
    residual = frames + gains[1] * branch_one
    normed_two, factor_two = layer_norm(residual)
    second = (normed_two * gains[2] + biases[4]).astype(jnp.bfloat16)
    hidden = jnp.einsum("bnd,df->bnf", second, w_fc1, preferred_element_type=jnp.float32) + fc1_bias
    active = gelu_value(hidden).astype(jnp.bfloat16)
    branch_two = (
        jnp.einsum("bnf,fd->bnd", active, w_fc2, preferred_element_type=jnp.float32) + biases[5]
    )
    output = (residual + gains[3] * branch_two).astype(jnp.bfloat16)
    kept = (
        normed_one,
        factor_one,
        normed_in,
        head_sets,
        visible_rows,
        log_total,
        token_outs,
        branch_one,
        normed_two,
        factor_two,
        second,
        hidden,
        active,
        branch_two,
    )
    return (output, kept)


def backward_layer(kept, cotangent, weight_set):
    w_qkv, w_proj, w_fc1, w_fc2, gains, biases, fc1_bias = weight_set
    (
        normed_one,
        factor_one,
        normed_in,
        head_sets,
        visible_rows,
        log_total,
        token_outs,
        branch_one,
        normed_two,
        factor_two,
        second,
        hidden,
        active,
        branch_two,
    ) = kept
    seq_count = lax.axis_size("seq")
    group_heads = H // seq_count
    group_width = D // seq_count
    image_count = cotangent.shape[0]
    local_rows = cotangent.shape[1]
    full_rows = local_rows * seq_count
    token_axes = (0, 1)
    upstream = cotangent.astype(jnp.float32)
    grad_branch = (gains[3] * upstream).astype(jnp.bfloat16)
    grad_scale_two = jnp.sum(branch_two * upstream, axis=token_axes)
    grad_bias_out = jnp.sum(grad_branch, axis=token_axes, dtype=jnp.float32)
    grad_down = jnp.einsum("bnf,bnd->fd", active, grad_branch, preferred_element_type=jnp.float32)
    grad_active = jnp.einsum("bnd,fd->bnf", grad_branch, w_fc2, preferred_element_type=jnp.float32)
    grad_hidden = (grad_active * gelu_slope(hidden)).astype(jnp.bfloat16)
    grad_bias_mid = jnp.sum(grad_hidden, axis=token_axes, dtype=jnp.float32)
    grad_upper = jnp.einsum("bnd,bnf->df", second, grad_hidden, preferred_element_type=jnp.float32)
    grad_second = jnp.einsum("bnf,df->bnd", grad_hidden, w_fc1, preferred_element_type=jnp.float32)
    grad_gain_two = jnp.sum(grad_second * normed_two, axis=token_axes)
    grad_shift_two = jnp.sum(grad_second, axis=token_axes)
    grad_resid = upstream + norm_back(grad_second * gains[2], normed_two, factor_two)
    grad_attend = (gains[1] * grad_resid).astype(jnp.bfloat16)
    grad_scale_one = jnp.sum(branch_one * grad_resid, axis=token_axes)
    grad_bias_proj = jnp.sum(grad_attend, axis=token_axes, dtype=jnp.float32)
    grad_outproj = jnp.einsum(
        "bnd,bne->de", token_outs, grad_attend, preferred_element_type=jnp.float32
    )
    grad_merged = jnp.einsum(
        "bne,de->bnd", grad_attend, w_proj, preferred_element_type=jnp.float32
    ).astype(jnp.bfloat16)
    head_grads_in = lax.all_to_all(
        grad_merged.reshape(image_count, local_rows, seq_count, group_width),
        "seq",
        split_axis=2,
        concat_axis=1,
        tiled=True,
    )
    head_upward = (
        head_grads_in.reshape(image_count, full_rows, group_heads, HD)
        .transpose(0, 2, 1, 3)
        .reshape(image_count * group_heads, full_rows, HD)
    )
    head_grads = lax.map(
        head_backward,
        (head_sets[0], head_sets[1], head_sets[2], visible_rows, log_total, head_upward),
    )
    stacked = (
        head_grads.reshape(image_count, group_heads, 3, full_rows, HD)
        .transpose(0, 3, 2, 1, 4)
        .reshape(image_count, full_rows, 3, group_width)
    )
    grad_packed = lax.all_to_all(stacked, "seq", split_axis=1, concat_axis=3, tiled=True).reshape(
        image_count, local_rows, 3 * D
    )
    grad_inproj = jnp.einsum(
        "bnd,bne->de", normed_in, grad_packed, preferred_element_type=jnp.float32
    )
    grad_bias_query = jnp.sum(grad_packed[..., :D], axis=token_axes, dtype=jnp.float32)
    grad_bias_value = jnp.sum(grad_packed[..., 2 * D :], axis=token_axes, dtype=jnp.float32)
    grad_entry = jnp.einsum("bne,de->bnd", grad_packed, w_qkv, preferred_element_type=jnp.float32)
    grad_gain_one = jnp.sum(grad_entry * normed_one, axis=token_axes)
    grad_shift_one = jnp.sum(grad_entry, axis=token_axes)
    grad_frames = grad_resid + norm_back(grad_entry * gains[0], normed_one, factor_one)
    gain_terms = jnp.stack([grad_gain_one, grad_scale_one, grad_gain_two, grad_scale_two])
    bias_terms = jnp.stack(
        [
            grad_shift_one,
            grad_bias_query,
            grad_bias_value,
            grad_bias_proj,
            grad_shift_two,
            grad_bias_out,
        ]
    )
    terms = (
        grad_inproj,
        grad_outproj,
        grad_upper,
        grad_down,
        gain_terms,
        bias_terms,
        grad_bias_mid,
    )
    return (grad_frames.astype(jnp.bfloat16), terms)


def per_device(images, key_mask, w_qkv, w_proj, w_fc1, w_fc2, gains, biases, fc1_bias, out_grad):
    section_zero = lax.axis_index("pipe") == 0
    image_count = images.shape[0] // MICRO
    visible_all = lax.all_gather(key_mask, "seq", axis=1, tiled=True) > 0
    gathered = (
        lax.all_gather(w_qkv, "dp", axis=1, tiled=True),
        lax.all_gather(w_proj, "dp", axis=1, tiled=True),
        lax.all_gather(w_fc1, "dp", axis=1, tiled=True),
        lax.all_gather(w_fc2, "dp", axis=1, tiled=True),
        lax.all_gather(gains.astype(jnp.bfloat16), "dp", axis=2, tiled=True).astype(gains.dtype),
        lax.all_gather(biases.astype(jnp.bfloat16), "dp", axis=2, tiled=True).astype(biases.dtype),
        lax.all_gather(fc1_bias.astype(jnp.bfloat16), "dp", axis=1, tiled=True).astype(
            fc1_bias.dtype
        ),
    )
    forward_set = tuple((tensor[0] for tensor in gathered))
    received = jnp.zeros((image_count, images.shape[1], D), jnp.bfloat16)
    produced = []
    stored = []
    for moment in range(MICRO + 1):
        if moment < MICRO:
            incoming = images[moment * image_count : (moment + 1) * image_count]
        else:
            incoming = jnp.zeros_like(received)
        current_slot = min(moment, MICRO - 1)
        earlier_slot = max(moment - 1, 0)
        visible = jnp.where(
            section_zero,
            visible_all[current_slot * image_count : (current_slot + 1) * image_count],
            visible_all[earlier_slot * image_count : (earlier_slot + 1) * image_count],
        )
        section_in = jnp.where(section_zero, incoming, received)
        output, kept = forward_layer(section_in, visible, forward_set)
        produced.append(output)
        stored.append(kept)
        if moment < MICRO:
            received = shifted_2(output, "pipe", 1)
    section_rows = [
        jnp.where(section_zero, produced[slot_index], produced[slot_index + 1])
        for slot_index in range(MICRO)
    ]
    section_outputs = jnp.concatenate(section_rows, axis=0)[None]
    regathered = (
        lax.all_gather(w_qkv, "dp", axis=1, tiled=True),
        lax.all_gather(w_proj, "dp", axis=1, tiled=True),
        lax.all_gather(w_fc1, "dp", axis=1, tiled=True),
        lax.all_gather(w_fc2, "dp", axis=1, tiled=True),
        lax.all_gather(gains.astype(jnp.bfloat16), "dp", axis=2, tiled=True).astype(gains.dtype),
        lax.all_gather(biases.astype(jnp.bfloat16), "dp", axis=2, tiled=True).astype(biases.dtype),
        lax.all_gather(fc1_bias.astype(jnp.bfloat16), "dp", axis=1, tiled=True).astype(
            fc1_bias.dtype
        ),
    )
    backward_set = tuple((tensor[0] for tensor in regathered))
    received_grad = jnp.zeros_like(received)
    grads_seen = []
    summed = None
    results = None
    for moment in range(MICRO + 1):
        slot_index = MICRO - 1 - moment
        if moment < MICRO:
            incoming = out_grad[slot_index * image_count : (slot_index + 1) * image_count]
        else:
            incoming = jnp.zeros_like(received)
        cotangent = jnp.where(section_zero, received_grad, incoming)
        input_grad, terms = backward_layer(stored[MICRO - moment], cotangent, backward_set)
        grads_seen.append(input_grad)
        if summed is None:
            summed = tuple(terms)
        else:
            summed = tuple((running + fresh_part for running, fresh_part in zip(summed, terms)))
        if moment < MICRO:
            received_grad = shifted_2(input_grad, "pipe", -1)
    results = (
        lax.psum_scatter(summed[0][None], ("seq", "dp"), scatter_dimension=1, tiled=True),
        lax.psum_scatter(summed[1][None], ("seq", "dp"), scatter_dimension=1, tiled=True),
        lax.psum_scatter(summed[2][None], ("seq", "dp"), scatter_dimension=1, tiled=True),
        lax.psum_scatter(summed[3][None], ("seq", "dp"), scatter_dimension=1, tiled=True),
        lax.psum_scatter(summed[4][None], ("seq", "dp"), scatter_dimension=2, tiled=True),
        lax.psum_scatter(summed[5][None], ("seq", "dp"), scatter_dimension=2, tiled=True),
        lax.psum_scatter(summed[6][None], ("seq", "dp"), scatter_dimension=1, tiled=True),
    )
    grad_rows = [
        jnp.where(section_zero, grads_seen[MICRO - slot_index], grads_seen[MICRO - 1 - slot_index])
        for slot_index in range(MICRO)
    ]
    input_grads = jnp.concatenate(grad_rows, axis=0)[None]
    return (
        section_outputs,
        input_grads,
        results[0],
        results[1],
        results[2],
        results[3],
        results[4],
        results[5],
        results[6],
    )


def solution(mesh):
    in_specs = (
        P("dp", "seq", None),
        P("dp", "seq"),
        P("pipe", "dp", None),
        P("pipe", "dp", None),
        P("pipe", "dp", None),
        P("pipe", "dp", None),
        P("pipe", None, "dp"),
        P("pipe", None, "dp"),
        P("pipe", "dp"),
        P("dp", "seq", None),
    )
    out_specs = (
        P("pipe", "dp", "seq", None),
        P("pipe", "dp", "seq", None),
        P("pipe", ("seq", "dp"), None),
        P("pipe", ("seq", "dp"), None),
        P("pipe", ("seq", "dp"), None),
        P("pipe", ("seq", "dp"), None),
        P("pipe", None, ("seq", "dp")),
        P("pipe", None, ("seq", "dp")),
        P("pipe", ("seq", "dp")),
    )
    return jax.shard_map(
        per_device, mesh=mesh, in_specs=in_specs, out_specs=out_specs, check_vma=False
    )
```

profile of v0, /device:TPU:10, one launch (start us, length us, event | category | flops | bytes accessed | tf_op | source)
XLA Modules:
  0.0 2596.3 jit_solution(12815897166140001238)
XLA Ops:
  9.5 8.1 all_gather.29
  17.6 7.4 all_gather.31
  26.8 54.4 %all-gather.6.cloned.1.call-done = bf16[1,1024,3072]{2,1,0:T(8,128)(2,1)} async-done(((bf16[1,256,3072]{2,1,0:T(8,128)(2,1)}), bf16[1,1024,3072]{2,1,0:T(8,128)(2,1)}) %all-gather.6.cloned.1.call-update) | async-done | bytes 6291472 | tf_op jit(solution)/shard_map/all_gather | solution.py:257
  81.2 6.7 add_convert_fusion.2
  99.3 51.7 %all-gather = s32[4,344,2]{1,2,0:T(2,128)S(1)} all-gather(s32[1,344,2]{1,2,0:T(2,128)S(1)} %bitcast.904), channel_id=1, replica_groups=mesh['pipe'=2,'seq'=4,'dp'=4] {'seq'}, dimensions={0}, use_global_device_ids=true | all-gather | bytes 13760 | tf_op jit(solution)/shard_map/all_gather | solution.py:255
  168.4 46.7 %while.66 = (s32[]{:T(128)}, bf16[4,1376,64]{1,2,0:T(8,128)(2,1)S(1)}, f32[4,1376]{1,0:T(4,128)}, pred[4,1376]{1,0:T(4,128)(4,1)}, bf16[4,1376,64]{2,1,0:T(8,128...) while((s32[]{:T(128)}, ...), condition=%wide.region_5.6_spmd, body=%wide.region_2.5_spmd.sunk | while | flops 499937952 | bytes 54528092 | solution.py:108
  218.9 8.4 reduce.68
  233.5 7.6 all_gather.35
  252.5 8.5 fusion.204
  261.1 36.3 %all-gather.12.cloned.1.call-done = bf16[1,4096,1024]{2,1,0:T(8,128)(2,1)} async-done(((bf16[1,1024,1024]{2,1,0:T(8,128)(2,1)}), bf16[1,4096,1024]{2,1,0:T(8,128)(2,1)}) %all-gather.12.cloned.1.call-update) | async-done | bytes 8388624 | tf_op jit(solution)/shard_map/all_gather | solution.py:260
  297.3 8.5 fusion.314
  310.2 6.7 add_convert_fusion.1
  328.0 45.8 %all-to-all-done.2 = bf16[1,344,3,4,256]{4,1,2,0,3:T(8,128)(2,1)S(1)} async-done(((bf16[1,344,3,4,256]{4,1,2,0,3:T(8,128)(2,1)}), bf16[1,344,3,4,256]{4,1,2,0,3:T(8,128)(2,1)S(1)}, u32[]{:S(2)}, u32[]{:S(2)}) %all-to-all-start.2) | async-done | bytes 2113568 | tf_op jit(solution)/shard_map/all_to_all | solution.py:95
  391.9 49.2 %while.67 = (s32[]{:T(128)}, bf16[4,1376,64]{1,2,0:T(8,128)(2,1)}, f32[4,1376]{1,0:T(4,128)}, pred[4,1376]{1,0:T(4,128)(4,1)}, bf16[4,1376,64]{2,1,0:T(8,128)(2,...) while((s32[]{:T(128)}, bf16[4,1376,64]{1,2,0:T(8,128)(2,1)}, ...), condition=%wide.region_13.14_spmd, body=%wide.region_10.13_spmd.sunk | while | flops 499937952 | bytes 54500672 | solution.py:108
  445.9 9.2 reduce.69
  457.0 23.3 all_to_all.180
  485.8 8.2 multiply_convert_fusion.4
  517.6 46.1 %all-to-all-done.4 = bf16[1,344,3,4,256]{4,1,2,0,3:T(8,128)(2,1)S(1)} async-done(((bf16[1,344,3,4,256]{4,1,2,0,3:T(8,128)(2,1)}), bf16[1,344,3,4,256]{4,1,2,0,3:T(8,128)(2,1)S(1)}, u32[]{:S(2)}, u32[]{:S(2)}) %all-to-all-start.4) | async-done | bytes 2113568 | tf_op jit(solution)/shard_map/all_to_all | solution.py:95
  580.4 42.0 %while.68 = (s32[]{:T(128)}, bf16[4,1376,64]{1,2,0:T(8,128)(2,1)S(1)}, f32[4,1376]{1,0:T(4,128)S(1)}, pred[4,1376]{1,0:T(4,128)(4,1)S(1)}, bf16[4,1376,64]{2,1,0...) while((s32[]{:T(128)}, ...), condition=%wide.region_21.22_spmd, body=%wide.region_18.21_spmd.sunk | while | flops 499937952 | bytes 54506048 | solution.py:108
  625.3 8.3 reduce.70
  634.6 23.9 all_to_all.181
  666.6 8.6 multiply_convert_fusion.3
  675.2 8.7 convert_reduce_fusion.2
  701.6 14.5 all-to-all-done.6
  721.5 101.8 %while.69 = (s32[]{:T(128)}, bf16[4,3,1376,64]{2,3,1,0:T(8,128)(2,1)}, pred[4,1376]{1,0:T(4,128)(4,1)S(1)}, bf16[4,1376,64]{2,1,0:T(8,128)(2,1)S(1)}, bf16[4,137...) while((s32[]{:T(128)}, ...), condition=%wide.region_28.29_spmd, body=%wide.region_26.28_spmd.sunk | while | flops 1230825088 | bytes 91117376 | solution.py:208
  724.5 6.4 multiply_reduce_fusion.15
  749.9 6.4 multiply_reduce_fusion.15
  775.4 6.4 multiply_reduce_fusion.15
  800.8 6.4 multiply_reduce_fusion.15
  828.6 68.6 %all_to_all.182 = bf16[1,1376,3,256]{3,2,0,1:T(4,128)(2,1)S(1)} all-to-all(bf16[1,1376,3,256]{3,2,0,1:T(4,128)(2,1)} %copy.189), channel_id=1, replica_groups=mesh['pipe'=2,'seq'=4,'dp'=4] {'seq'}, dimensions={1} | all-to-all | bytes 4227072 | tf_op jit(solution)/shard_map/all_to_all | solution.py:217
  901.3 6.8 fusion.274
  915.1 8.9 convert_reduce_fusion.1
  939.6 15.6 all-to-all-done.8
  959.1 104.5 %while.70 = (s32[]{:T(128)}, bf16[4,3,1376,64]{2,3,1,0:T(8,128)(2,1)}, pred[4,1376]{1,0:T(4,128)(4,1)}, bf16[4,1376,64]{2,1,0:T(8,128)(2,1)S(1)}, bf16[4,1376,64...) while((s32[]{:T(128)}, ...), condition=%wide.region_35.36_spmd, body=%wide.region_33.35_spmd.sunk | while | flops 1230825088 | bytes 91117376 | solution.py:208
  962.8 6.4 multiply_reduce_fusion.16
  988.9 6.4 multiply_reduce_fusion.16
  1015.0 6.4 multiply_reduce_fusion.16
  1041.1 6.4 multiply_reduce_fusion.16
  1071.4 68.0 %all_to_all.183 = bf16[1,1376,3,256]{3,2,0,1:T(4,128)(2,1)S(1)} all-to-all(bf16[1,1376,3,256]{3,2,0,1:T(4,128)(2,1)S(1)} %copy.199), channel_id=1, replica_groups=mesh['pipe'=2,'seq'=4,'dp'=4] {'seq'}, dimensions={1} | all-to-all | bytes 4227072 | tf_op jit(solution)/shard_map/all_to_all | solution.py:217
  1143.4 6.7 fusion.283
  1154.8 7.6 fusion.336
  1162.4 8.0 convert_reduce_fusion
  1181.4 22.4 all_to_all.184
  1206.9 100.6 %while.71 = (s32[]{:T(128)}, bf16[4,3,1376,64]{2,3,1,0:T(8,128)(2,1)}, pred[4,1376]{1,0:T(4,128)(4,1)}, bf16[4,1376,64]{2,1,0:T(8,128)(2,1)S(1)}, bf16[4,1376,64...) while((s32[]{:T(128)}, ...), condition=%wide.region_42.43_spmd, body=%wide.region_40.42_spmd.sunk | while | flops 1230825088 | bytes 91292992 | solution.py:208
  1235.6 6.4 multiply_reduce_fusion.17
  1260.8 6.4 multiply_reduce_fusion.17
  1285.9 6.4 multiply_reduce_fusion.17
  1312.9 6.4 all-to-all-start.11
  1340.8 39.4 %all-to-all-done.11 = bf16[1,1376,3,256]{3,2,0,1:T(4,128)(2,1)} async-done(((bf16[1,1376,3,256]{3,2,0,1:T(4,128)(2,1)}), bf16[1,1376,3,256]{3,2,0,1:T(4,128)(2,1)}, u32[]{:S(2)}, u32[]{:S(2)}) %all-to-all-start.11) | async-done | bytes 2113568 | tf_op jit(solution)/shard_map/all_to_all | solution.py:217
  1388.9 6.8 fusion.292
  1405.6 6.9 add_bitcast_fusion.3
  1419.2 6.7 fusion.370
  1425.8 14.1 add_bitcast_fusion.2
  1441.3 10.2 fusion.354
  1451.5 8.2 fusion.348
  1459.7 21.1 add_bitcast_fusion
  1482.2 10.3 fusion.378
  1492.6 8.5 fusion.381
  1501.1 20.1 add_bitcast_fusion.1
  1530.2 34.7 %reduce-scatter.24.cloned.1.call-done = f32[64,6]{1,0:T(8,128)} async-done(((f32[1024,6]{1,0:T(8,128)}), f32[64,6]{1,0:T(8,128)}) %reduce-scatter.24.cloned.1.call-update) | async-done | bytes 1552
  1566.6 103.2 %reduce-scatter.16.cloned.1.call-done = f32[1,64,1024]{2,1,0:T(8,128)} async-done(((f32[1,1024,1024]{2,1,0:T(8,128)}), f32[1,64,1024]{2,1,0:T(8,128)}) %reduce-scatter.16.cloned.1.call-update) | async-done | bytes 262160 | tf_op jit(solution)/shard_map/reduce_scatter | solution.py:327
  1669.8 210.3 %reduce-scatter.14.cloned.1.call-done = f32[1,64,3072]{2,1,0:T(8,128)} async-done(((f32[1,1024,3072]{2,1,0:T(8,128)}), f32[1,64,3072]{2,1,0:T(8,128)}) %reduce-scatter.14.cloned.1.call-update) | async-done | bytes 786448 | tf_op jit(solution)/shard_map/reduce_scatter | solution.py:326
  1880.0 354.4 %reduce-scatter.20.cloned.1.call-done = f32[1,256,1024]{2,1,0:T(8,128)} async-done(((f32[1,4096,1024]{2,1,0:T(8,128)}), f32[1,256,1024]{2,1,0:T(8,128)}) %reduce-scatter.20.cloned.1.call-update) | async-done | bytes 1048592 | tf_op jit(solution)/shard_map/reduce_scatter | solution.py:329
  2234.5 355.0 %reduce-scatter.18.cloned.1.call-done = f32[1,64,4096]{2,1,0:T(8,128)} async-done(((f32[1,1024,4096]{2,1,0:T(8,128)}), f32[1,64,4096]{2,1,0:T(8,128)}) %reduce-scatter.18.cloned.1.call-update) | async-done | bytes 1048592 | tf_op jit(solution)/shard_map/reduce_scatter | solution.py:328
  (870 shorter events, 679.1 us)
Async XLA Ops:
  7.2 74.0 %all-gather.6.cloned.1.call-start = ((), (), s32[]{:S(2)}) async-start(), calls=%async_computation.19 | async-start | bytes 7864320 | tf_op jit(solution)/shard_map/all_gather | solution.py:257
  7.9 17.6 copy-start.36
  7.9 239.3 %all-gather.8.cloned.1.call-start = ((), (), s32[]{:S(2)}) async-start(), calls=%async_computation.20 | async-start | bytes 2621440 | tf_op jit(solution)/shard_map/all_gather | solution.py:258
  8.7 243.4 %all-gather.10.cloned.1.call-start = ((), (), s32[]{:S(2)}) async-start(), calls=%async_computation.21 | async-start | bytes 10485760 | tf_op jit(solution)/shard_map/all_gather | solution.py:259
  25.6 55.7 %copy-start.89 = (f32[1,1,1024]{2,0,1:T(1,128)}, f32[1,1,1024]{2,0,1:T(1,128)S(1)}, u32[]{:S(2)}) copy-start(f32[1,1,1024]{2,0,1:T(1,128)S(1)} %get-tuple-element.621) | copy-start | bytes 12292
  25.6 55.6 %copy-start.162 = (f32[3072]{0:T(1024)}, f32[3072]{0:T(1024)S(1)}, u32[]{:S(2)}) copy-start(f32[3072]{0:T(1024)S(1)} %pad_maximum_fusion) | copy-start | bytes 36868
  25.8 55.4 %copy-start.129 = (f32[344]{0:T(512)}, f32[344]{0:T(512)S(1)}, u32[]{:S(2)}) copy-start(f32[344]{0:T(512)S(1)} %broadcast_multiply_fusion.17) | copy-start | bytes 4132
  26.2 55.0 %copy-start.134 = (f32[344]{0:T(512)}, f32[344]{0:T(512)S(1)}, u32[]{:S(2)}) copy-start(f32[344]{0:T(512)S(1)} %add_rsqrt_fusion.5) | copy-start | bytes 4132
  26.8 475.7 %copy-start.78 = (f32[1,1,1024]{2,1,0:T(1,128)}, f32[1,1,1024]{2,1,0:T(1,128)S(1)}, u32[]{:S(2)}) copy-start(f32[1,1,1024]{2,1,0:T(1,128)S(1)} %get-tuple-element.627) | copy-start | bytes 12292
  26.8 1148.3 %copy-start.81 = (f32[1,1,1024]{2,1,0:T(1,128)}, f32[1,1,1024]{2,1,0:T(1,128)S(1)}, u32[]{:S(2)}) copy-start(f32[1,1,1024]{2,1,0:T(1,128)S(1)} %get-tuple-element.625) | copy-start | bytes 12292
  93.5 58.3 %all-to-all-start = ((bf16[1,344,3,4,256]{4,1,2,0,3:T(8,128)(2,1)}), bf16[1,344,3,4,256]{4,1,2,0,3:T(8,128)(2,1)S(1)}, u32[]{:S(2)}, u32[]{:S(2)}) async-start(bf16[1,344,3,4,256]{4,1,2,0,3:T(8,128)(2,1)} %copy.161), calls=%async_computation | async-start | bytes 4227072 | tf_op jit(solution)/shard_map/all_to_all | solution.py:95
  98.6 198.7 %all-gather.12.cloned.1.call-start = ((), (), s32[]{:S(2)}) async-start(), calls=%async_computation.22 | async-start | bytes 10485760 | tf_op jit(solution)/shard_map/all_gather | solution.py:260
  215.1 12.2 copy-start.6
  215.2 12.2 copy-start.8
  228.3 17.7 all-to-all-start.1
  251.7 45.6 %copy-start.26 = (f32[1,344,1024]{2,1,0:T(8,128)}, f32[1,344,1024]{2,1,0:T(8,128)S(1)}, u32[]{:S(2)}) copy-start(f32[1,344,1024]{2,1,0:T(8,128)S(1)} %get-tuple-element.591) | copy-start | bytes 4227076
  251.8 9.3 copy-start.131
  252.1 9.0 copy-start.136
  252.5 44.8 %copy-start.97 = (f32[1,1,1024]{2,1,0:T(1,128)S(1)}, f32[1,1,1024]{2,1,0:T(1,128)}, u32[]{:S(2)}) copy-start(f32[1,1,1024]{2,1,0:T(1,128)} %get-tuple-element.624) | copy-start | bytes 12292
  252.5 44.8 %copy-start.169 = (f32[1,1,1024]{2,0,1:T(1,128)S(1)}, f32[1,1,1024]{2,0,1:T(1,128)}, u32[]{:S(2)}) copy-start(f32[1,1,1024]{2,0,1:T(1,128)} %get-tuple-element.619) | copy-start | bytes 12292
  305.9 3.7 collective-permute-start
  309.8 171.7 %copy-start.29 = (bf16[1,344,1024]{2,1,0:T(8,128)(2,1)}, bf16[1,344,1024]{2,1,0:T(8,128)(2,1)S(1)}, u32[]{:S(2)}) copy-start(bf16[1,344,1024]{2,1,0:T(8,128)(2,1)S(1)} %get-tuple-element.589) | copy-start | bytes 2113540
  322.4 51.3 %all-to-all-start.2 = ((bf16[1,344,3,4,256]{4,1,2,0,3:T(8,128)(2,1)}), bf16[1,344,3,4,256]{4,1,2,0,3:T(8,128)(2,1)S(1)}, u32[]{:S(2)}, u32[]{:S(2)}) async-start(bf16[1,344,3,4,256]{4,1,2,0,3:T(8,128)(2,1)} %copy.168), calls=%async_computation.2 | async-start | bytes 4227072 | tf_op jit(solution)/shard_map/all_to_all | solution.py:95
  441.1 14.0 copy-start.9
  441.1 14.0 copy-start.11
  482.9 11.1 slice-start.8
  485.0 9.0 copy-start.16
  485.0 8.9 copy-start.109
  498.7 3.2 collective-permute-start.1
  501.9 406.9 %copy-start.32 = (bf16[1,344,1024]{2,1,0:T(8,128)(2,1)}, bf16[1,344,1024]{2,1,0:T(8,128)(2,1)S(1)}, u32[]{:S(2)}) copy-start(bf16[1,344,1024]{2,1,0:T(8,128)(2,1)S(1)} %collective-permute-done.1) | copy-start | bytes 2113540
  512.2 51.5 %all-to-all-start.4 = ((bf16[1,344,3,4,256]{4,1,2,0,3:T(8,128)(2,1)}), bf16[1,344,3,4,256]{4,1,2,0,3:T(8,128)(2,1)S(1)}, u32[]{:S(2)}, u32[]{:S(2)}) async-start(bf16[1,344,3,4,256]{4,1,2,0,3:T(8,128)(2,1)} %copy.175), calls=%async_computation.4 | async-start | bytes 4227072 | tf_op jit(solution)/shard_map/all_to_all | solution.py:95
  622.4 11.2 copy-start.96
  665.9 22.7 copy-start.19
  665.9 22.7 copy-start.107
  666.6 22.0 copy-start.122
  666.6 17.4 slice-start.2
  696.4 19.7 all-to-all-start.6
  909.4 14.5 slice-start.4
  910.7 4.2 collective-permute-start.2
  915.0 260.1 %copy-start.34 = (bf16[1,344,1024]{2,1,0:T(8,128)(2,1)}, bf16[1,344,1024]{2,1,0:T(8,128)(2,1)S(1)}, u32[]{:S(2)}) copy-start(bf16[1,344,1024]{2,1,0:T(8,128)(2,1)S(1)} %slice_select_fusion) | copy-start | bytes 2113540
  915.0 8.9 copy-start.17
  915.0 8.9 copy-start.110
  915.0 8.9 copy-start.125
  934.2 21.0 all-to-all-start.8
  1143.4 11.3 copy-start.171
  1151.5 10.9 slice-start
  1153.1 9.3 copy-start.61
  1153.1 9.3 collective-permute-start.3
  1154.8 15.7 slice-start.6
  1162.4 12.7 copy-start.58
  1312.9 67.3 %all-to-all-start.11 = ((bf16[1,1376,3,256]{3,2,0,1:T(4,128)(2,1)}), bf16[1,1376,3,256]{3,2,0,1:T(4,128)(2,1)}, u32[]{:S(2)}, u32[]{:S(2)}) async-start(bf16[1,1376,3,256]{3,2,0,1:T(4,128)(2,1)} %copy.209), calls=%async_computation.11 | async-start | bytes 5636096 | tf_op jit(solution)/shard_map/all_to_all | solution.py:217
  1319.3 204.6 %reduce-scatter.26.cloned.1.call-start = ((), (), s32[]{:S(2)}) async-start(), calls=%async_computation.29 | async-start | bytes 2228224
  1338.7 190.2 %reduce-scatter.22.cloned.1.call-start = ((), (), s32[]{:S(2)}) async-start(), calls=%async_computation.27 | async-start | bytes 557056
  1401.2 163.8 %reduce-scatter.24.cloned.1.call-start = ((), (), s32[]{:S(2)}) async-start(), calls=%async_computation.28 | async-start | bytes 557056
  1405.5 264.2 %reduce-scatter.16.cloned.1.call-start = ((), (), s32[]{:S(2)}) async-start(), calls=%async_computation.24 | async-start | bytes 4456448 | tf_op jit(solution)/shard_map/reduce_scatter | solution.py:327
  1412.6 467.4 %reduce-scatter.14.cloned.1.call-start = ((), (), s32[]{:S(2)}) async-start(), calls=%async_computation.23 | async-start | bytes 13369344 | tf_op jit(solution)/shard_map/reduce_scatter | solution.py:326
  1440.0 11.5 copy-start.35
  1440.0 794.5 %reduce-scatter.20.cloned.1.call-start = ((), (), s32[]{:S(2)}) async-start(), calls=%async_computation.26 | async-start | bytes 17825792 | tf_op jit(solution)/shard_map/reduce_scatter | solution.py:329
  1441.3 10.2 copy-start.52
  1480.9 11.6 copy-start.18
  1480.9 11.6 copy-start.111
  1480.9 11.6 copy-start.126
  1480.9 1108.6 %reduce-scatter.18.cloned.1.call-start = ((), (), s32[]{:S(2)}) async-start(), calls=%async_computation.25 | async-start | bytes 17825792 | tf_op jit(solution)/shard_map/reduce_scatter | solution.py:328
  1482.2 10.3 copy-start.72
  (183 other events, 651.3 us)
Sparse Core Ops, SparseCore 0:
  9.9 71.3 all-gather.5
  83.0 35.2 all-gather.7
  120.2 87.6 all-gather.9
  209.6 87.6 all-gather.11
  1338.8 83.1 reduce-scatter.25
  1424.1 65.5 reduce-scatter.21
  1492.1 72.8 reduce-scatter.23
  1567.9 101.8 reduce-scatter.15
  1676.0 203.9 reduce-scatter.13
  1882.9 351.5 reduce-scatter.19
  2237.5 351.9 reduce-scatter.17
where the time goes:
time: 2610 us; the launch traced here: 2600 us
  waiting for transfers between devices  1320 us (51%)
  matrix products  536 us (21%)
  blocking collectives  281 us (11%)
  local copies, waits for them, and re-layouts  237 us (9%)
  other arithmetic  156 us (6%)
  starting transfers between devices  46.3 us (2%)
    reduce_scatter x1, waiting for transfers between devices, per_device(): lax.psum_scatter(summed[2][None], ('seq', 'dp'), scatter_dimension=1, til...  355 us
    reduce_scatter x1, waiting for transfers between devices, per_device(): lax.psum_scatter(summed[3][None], ('seq', 'dp'), scatter_dimension=1, til...  354 us
    reduce_scatter x1, waiting for transfers between devices, per_device(): lax.psum_scatter(summed[0][None], ('seq', 'dp'), scatter_dimension=1, til...  210 us
    all_to_all x2, blocking collectives, backward_layer(): lax.all_to_all(stacked, 'seq', split_axis=1, concat_axis=3, tiled=True)  137 us
    reduce_scatter x1, waiting for transfers between devices, per_device(): lax.psum_scatter(summed[1][None], ('seq', 'dp'), scatter_dimension=1, til...  103 us
    dot_general x24, matrix products, masked_scores(): jnp.dot(queries, key_rows.T, preferred_element_type=jnp.float32) * 0.125  96.9 us
    all_to_all x3, waiting for transfers between devices, forward_layer(): lax.all_to_all(packed.reshape(image_count, local_rows, 3, seq_count, grou...  91.8 us
    convert_element_type x12, other arithmetic, head_backward(): score_grads = (attention * centred).astype(jnp.bfloat16)  74.8 us
  transfers between devices with their start and end apart: 22, of which 16 were waited for; matrix products, arithmetic and copies ran while one was open for 10% of the time, Pallas kernels for 0%

commit v1 on v0

v1 whole, which is shorter than its diff:
```python
import functools

import jax
import jax.numpy as jnp
from jax import lax
from jax.experimental import pallas as pl
from jax.experimental.pallas import tpu as pltpu
from jax.sharding import PartitionSpec as P

D = 1024
H = 16
HD = 64

epsilon = 1e-06
root_half = 0.7071067811865476
inv_root_tau = 0.3989422804014327
ALL = ("seq", "dp", "pipe")
F32 = jnp.float32
BF16 = jnp.bfloat16


def layer_norm(values):
    centre = jnp.mean(values, axis=-1, keepdims=True)
    shifted = values - centre
    factor = lax.rsqrt(jnp.mean(shifted * shifted, axis=-1, keepdims=True) + epsilon)
    return (shifted * factor, factor)


def norm_back(upward, normed, factor):
    inner = (
        upward
        - jnp.mean(upward, axis=-1, keepdims=True)
        - normed * jnp.mean(upward * normed, axis=-1, keepdims=True)
    )
    return factor * inner


def gelu_value(hidden):
    return 0.5 * hidden * (1.0 + lax.erf(hidden * root_half))


def gelu_slope(hidden):
    return (
        0.5 * (1.0 + lax.erf(hidden * root_half))
        + hidden * jnp.exp(-0.5 * hidden * hidden) * inv_root_tau
    )


def swap(block):
    return lax.ppermute(block, "pipe", [(0, 1), (1, 0)])


def to_sections(first, second, axis):
    low = lax.axis_index("pipe") == 0
    mine = jnp.where(low, first, second)
    theirs = swap(jnp.where(low, second, first))
    return jnp.where(
        low,
        jnp.concatenate([mine, theirs], axis=axis),
        jnp.concatenate([theirs, mine], axis=axis),
    )


NT = (((1,), (1,)), ((), ()))
NN = (((1,), (0,)), ((), ()))
TN = (((0,), (0,)), ((), ()))


def dot(a, b, dims):
    return lax.dot_general(a, b, dims, preferred_element_type=F32)


def forward_kernel(heads, q_ref, k_ref, v_ref, bias_ref, o_ref, lse_ref):
    bias = bias_ref[0]
    outs, sums = [], []
    for h in range(heads):
        cols = slice(h * HD, (h + 1) * HD)
        s = dot(q_ref[0, :, cols] * jnp.asarray(0.125, BF16), k_ref[0, :, cols], NT) + bias
        highest = jnp.max(s, axis=-1, keepdims=True)
        w = jnp.exp(s - highest)
        total = jnp.sum(w, axis=-1, keepdims=True)
        o = dot(w.astype(BF16), v_ref[0, :, cols], NN) / total
        outs.append(o.astype(BF16))
        sums.append(highest + jnp.log(total))
    o_ref[0] = jnp.concatenate(outs, axis=-1)
    lse_ref[0] = jnp.concatenate(sums, axis=-1)


def attention_forward(q, k, v, bias_row, block):
    count, rows, width = q.shape
    heads = width // HD
    steps = rows // block
    some = pl.BlockSpec((1, block, width), lambda b, i: (b, i, 0))
    whole = pl.BlockSpec((1, rows, width), lambda b, i: (b, 0, 0))
    return pl.pallas_call(
        functools.partial(forward_kernel, heads),
        grid=(count, steps),
        in_specs=[some, whole, whole, pl.BlockSpec((1, 1, rows), lambda b, i: (b, 0, 0))],
        out_specs=[some, pl.BlockSpec((1, block, heads), lambda b, i: (b, i, 0))],
        out_shape=[
            jax.ShapeDtypeStruct((count, rows, width), BF16),
            jax.ShapeDtypeStruct((count, rows, heads), F32),
        ],
        compiler_params=pltpu.CompilerParams(vmem_limit_bytes=48 << 20),
        cost_estimate=pl.CostEstimate(
            flops=4 * count * rows * rows * width,
            bytes_accessed=8 * count * rows * width,
            transcendentals=count * heads * rows * rows,
        ),
    )(q, k, v, bias_row)


def backward_kernel(
    heads, q_ref, k_ref, v_ref, bias_ref, lse_ref, delta_ref, do_ref,
    dq_ref, dk_ref, dv_ref, dk_sum, dv_sum,
):
    step = pl.program_id(1)

    @pl.when(step == 0)
    def _():
        dk_sum[...] = jnp.zeros_like(dk_sum)
        dv_sum[...] = jnp.zeros_like(dv_sum)

    bias = bias_ref[0]
    dqs, dks, dvs = [], [], []
    for h in range(heads):
        cols = slice(h * HD, (h + 1) * HD)
        q = q_ref[0, :, cols] * jnp.asarray(0.125, BF16)
        k = k_ref[0, :, cols]
        do = do_ref[0, :, cols]
        s = dot(k, q, NT) + bias
        p = jnp.exp(s - lse_ref[0, 0, h : h + 1, :])
        dp = dot(v_ref[0, :, cols], do, NT)
        ds = (p * (dp - delta_ref[0, 0, h : h + 1, :])).astype(BF16)
        dqs.append(dot(ds, k, TN) * 0.125)
        dks.append(dot(ds, q, NN))
        dvs.append(dot(p.astype(BF16), do, NN))
    dq_ref[0] = jnp.concatenate(dqs, axis=-1).astype(BF16)
    dk_sum[...] += jnp.concatenate(dks, axis=-1)
    dv_sum[...] += jnp.concatenate(dvs, axis=-1)

    @pl.when(step == pl.num_programs(1) - 1)
    def _():
        dk_ref[0] = dk_sum[...].astype(BF16)
        dv_ref[0] = dv_sum[...].astype(BF16)


def attention_backward(q, k, v, bias_column, lse, delta, do, block):
    count, rows, width = q.shape
    heads = width // HD
    steps = rows // block
    some = pl.BlockSpec((1, block, width), lambda b, i: (b, i, 0))
    whole = pl.BlockSpec((1, rows, width), lambda b, i: (b, 0, 0))
    lines = pl.BlockSpec((1, 1, heads, block), lambda b, i: (b, i, 0, 0))

    def as_lines(values):
        return values.reshape(count, steps, block, heads).transpose(0, 1, 3, 2)

    shape = jax.ShapeDtypeStruct((count, rows, width), BF16)
    return pl.pallas_call(
        functools.partial(backward_kernel, heads),
        grid=(count, steps),
        in_specs=[
            some, whole, whole, pl.BlockSpec((1, rows, 1), lambda b, i: (b, 0, 0)),
            lines, lines, some,
        ],
        out_specs=[some, whole, whole],
        out_shape=[shape, shape, shape],
        scratch_shapes=[pltpu.VMEM((rows, width), F32), pltpu.VMEM((rows, width), F32)],
        compiler_params=pltpu.CompilerParams(vmem_limit_bytes=48 << 20),
        cost_estimate=pl.CostEstimate(
            flops=10 * count * rows * rows * width,
            bytes_accessed=14 * count * rows * width,
            transcendentals=count * heads * rows * rows,
        ),
    )(q, k, v, bias_column, as_lines(lse), as_lines(delta), do)


def forward_layer(section_in, hidden_keys, weight_set):
    w_qkv, w_proj, w_fc1, w_fc2, gains, biases, fc1_bias = weight_set
    seq_count = lax.axis_size("seq")
    group_width = D // seq_count
    image_count, local_rows = section_in.shape[:2]
    full_rows = local_rows * seq_count
    frames = section_in.astype(F32)
    normed_one, factor_one = layer_norm(frames)
    normed_in = (normed_one * gains[0] + biases[0]).astype(BF16)
    projected = jnp.einsum("bnd,de->bne", normed_in, w_qkv, preferred_element_type=F32)
    bias_row = jnp.concatenate([biases[1], jnp.zeros_like(biases[1]), biases[2]])
    packed = (projected + bias_row).astype(BF16)
    spread = lax.all_to_all(
        packed.reshape(image_count, local_rows, 3, seq_count, group_width),
        "seq",
        split_axis=3,
        concat_axis=1,
        tiled=True,
    ).reshape(image_count, full_rows, 3, group_width)
    head_sets = (spread[:, :, 0], spread[:, :, 1], spread[:, :, 2])
    merged, log_total = attention_forward(
        *head_sets, hidden_keys[:, None, :], local_rows
    )
    token_outs = lax.all_to_all(merged, "seq", split_axis=1, concat_axis=2, tiled=True)
    branch_one = jnp.einsum("bnd,de->bne", token_outs, w_proj, preferred_element_type=F32) + biases[3]
    residual = frames + gains[1] * branch_one
    normed_two, factor_two = layer_norm(residual)
    second = (normed_two * gains[2] + biases[4]).astype(BF16)
    hidden = jnp.einsum("bnd,df->bnf", second, w_fc1, preferred_element_type=F32) + fc1_bias
    active = gelu_value(hidden).astype(BF16)
    branch_two = jnp.einsum("bnf,fd->bnd", active, w_fc2, preferred_element_type=F32) + biases[5]
    output = (residual + gains[3] * branch_two).astype(BF16)
    kept = (
        normed_one, factor_one, normed_in, head_sets, merged, log_total, token_outs,
        branch_one, normed_two, factor_two, second, hidden, active, branch_two,
    )
    return (output, kept)


def backward_layer(kept, cotangent, hidden_keys, weight_set):
    w_qkv, w_proj, w_fc1, w_fc2, gains, biases, fc1_bias = weight_set
    (
        normed_one, factor_one, normed_in, head_sets, merged, log_total, token_outs,
        branch_one, normed_two, factor_two, second, hidden, active, branch_two,
    ) = kept
    seq_count = lax.axis_size("seq")
    group_width = D // seq_count
    image_count, local_rows = cotangent.shape[:2]
    full_rows = local_rows * seq_count
    token_axes = (0, 1)

    def total(values):
        return jnp.sum(values, axis=token_axes, dtype=F32)

    def weight_grad(left, right):
        whole = jnp.einsum("bnd,bne->de", left, right, preferred_element_type=F32)
        return lax.psum_scatter(whole.astype(BF16), ALL, scatter_dimension=0, tiled=True)

    upstream = cotangent.astype(F32)
    grad_branch = (gains[3] * upstream).astype(BF16)
    grad_scale_two = total(branch_two * upstream)
    grad_bias_out = total(grad_branch)
    grad_down = weight_grad(active, grad_branch)
    grad_active = jnp.einsum("bnd,fd->bnf", grad_branch, w_fc2, preferred_element_type=F32)
    grad_hidden = (grad_active * gelu_slope(hidden)).astype(BF16)
    grad_bias_mid = total(grad_hidden)
    grad_upper = weight_grad(second, grad_hidden)
    grad_second = jnp.einsum("bnf,df->bnd", grad_hidden, w_fc1, preferred_element_type=F32)
    grad_gain_two = total(grad_second * normed_two)
    grad_shift_two = total(grad_second)
    grad_resid = upstream + norm_back(grad_second * gains[2], normed_two, factor_two)
    grad_attend = (gains[1] * grad_resid).astype(BF16)
    grad_scale_one = total(branch_one * grad_resid)
    grad_bias_proj = total(grad_attend)
    grad_outproj = weight_grad(token_outs, grad_attend)
    grad_merged = jnp.einsum(
        "bne,de->bnd", grad_attend, w_proj, preferred_element_type=F32
    ).astype(BF16)
    head_upward = lax.all_to_all(
        grad_merged.reshape(image_count, local_rows, seq_count, group_width),
        "seq",
        split_axis=2,
        concat_axis=1,
        tiled=True,
    ).reshape(image_count, full_rows, group_width)
    delta = jnp.sum(
        (head_upward.astype(F32) * merged.astype(F32)).reshape(image_count, full_rows, -1, HD),
        axis=-1,
    )
    head_grads = attention_backward(
        *head_sets, hidden_keys[:, :, None], log_total, delta, head_upward, local_rows
    )
    grad_packed = lax.all_to_all(
        jnp.stack(head_grads, axis=2), "seq", split_axis=1, concat_axis=3, tiled=True
    ).reshape(image_count, local_rows, 3 * D)
    grad_inproj = weight_grad(normed_in, grad_packed)
    grad_bias_query = total(grad_packed[..., :D])
    grad_bias_value = total(grad_packed[..., 2 * D :])
    grad_entry = jnp.einsum("bne,de->bnd", grad_packed, w_qkv, preferred_element_type=F32)
    grad_gain_one = total(grad_entry * normed_one)
    grad_shift_one = total(grad_entry)
    grad_frames = grad_resid + norm_back(grad_entry * gains[0], normed_one, factor_one)
    rows = jnp.stack(
        [
            grad_gain_one, grad_scale_one, grad_gain_two, grad_scale_two,
            grad_shift_one, grad_bias_query, grad_bias_value, grad_bias_proj,
            grad_shift_two, grad_bias_out,
        ]
    )
    return (
        grad_frames.astype(BF16),
        (grad_inproj, grad_outproj, grad_upper, grad_down),
        (rows, grad_bias_mid),
    )


def per_device(images, key_mask, w_qkv, w_proj, w_fc1, w_fc2, gains, biases, fc1_bias, out_grad):
    core = lax.axis_index("pipe")
    low = core == 0
    dp_count = lax.axis_size("dp")
    shards = lax.axis_size("seq") * dp_count
    image_count = images.shape[0] // lax.axis_size("pipe")

    def my_images(array):
        return lax.dynamic_slice_in_dim(array, core * image_count, image_count, axis=0)

    part = gains.shape[2]
    small = jnp.concatenate([gains[0], biases[0], fc1_bias[0].reshape(-1, part)], axis=0)
    small = lax.all_gather(small, ("pipe", "dp"), axis=0)
    visible = lax.all_gather(my_images(key_mask), "seq", axis=1, tiled=True) > 0
    hidden_keys = jnp.where(visible, 0.0, -1e30).astype(F32)

    halves = []
    for tensor in (w_qkv[0], w_proj[0], w_fc1[0], w_fc2[0]):
        half = tensor.shape[0] // 2
        keep = lax.dynamic_slice_in_dim(tensor, core * half, half, axis=0)
        received = swap(lax.dynamic_slice_in_dim(tensor, (1 - core) * half, half, axis=0))
        halves.append((jnp.where(low, keep, received), jnp.where(low, received, keep)))

    sets = []
    for layer in range(2):
        rest = small[layer * dp_count : (layer + 1) * dp_count]
        lines = rest[:, :10].transpose(1, 0, 2).reshape(10, D)
        mids = rest[:, 10:].reshape(-1)
        whole = tuple(
            lax.all_gather(pair[layer], ("dp", "pipe"), axis=0, tiled=True) for pair in halves
        )
        sets.append((*whole, lines[:4], lines[4:], mids))

    middle, kept_zero = forward_layer(my_images(images), hidden_keys, sets[0])
    final, kept_one = forward_layer(middle, hidden_keys, sets[1])
    section_outputs = to_sections(middle, final, 0)[None]
    grad_middle, weights_one, vectors_one = backward_layer(
        kept_one, my_images(out_grad), hidden_keys, sets[1]
    )
    grad_first, weights_zero, vectors_zero = backward_layer(
        kept_zero, grad_middle, hidden_keys, sets[0]
    )
    input_grads = to_sections(grad_first, grad_middle, 0)[None]

    packed = []
    for rows, mids in (vectors_zero, vectors_one):
        lines = rows.reshape(10, shards, -1).transpose(1, 0, 2).reshape(shards, -1)
        packed.append(jnp.concatenate([lines, mids.reshape(shards, -1)], axis=1))
    mine = lax.psum_scatter(
        jnp.concatenate(packed, axis=0), ("pipe", "seq", "dp"), scatter_dimension=0, tiled=True
    )[0]
    width = D // shards
    lines = mine[: 10 * width].reshape(10, width)
    weights = [
        to_sections(zero, one, 0).astype(F32)[None]
        for zero, one in zip(weights_zero, weights_one)
    ]
    return (
        section_outputs,
        input_grads,
        *weights,
        lines[:4][None],
        lines[4:][None],
        mine[10 * width :][None],
    )


def solution(mesh):
    in_specs = (
        P("dp", "seq", None),
        P("dp", "seq"),
        P("pipe", "dp", None),
        P("pipe", "dp", None),
        P("pipe", "dp", None),
        P("pipe", "dp", None),
        P("pipe", None, "dp"),
        P("pipe", None, "dp"),
        P("pipe", "dp"),
        P("dp", "seq", None),
    )
    out_specs = (
        P("pipe", "dp", "seq", None),
        P("pipe", "dp", "seq", None),
        P("pipe", ("seq", "dp"), None),
        P("pipe", ("seq", "dp"), None),
        P("pipe", ("seq", "dp"), None),
        P("pipe", ("seq", "dp"), None),
        P("pipe", None, ("seq", "dp")),
        P("pipe", None, ("seq", "dp")),
        P("pipe", ("seq", "dp")),
    )
    return jax.shard_map(
        per_device, mesh=mesh, in_specs=in_specs, out_specs=out_specs, check_vma=False
    )
```

time: 2610 us -> 1800 us (0.69)
  matrix products: 536 us -> 159 us
  waiting for transfers between devices: 1320 us -> 1140 us
  blocking collectives: 281 us -> 121 us
  local copies, waits for them, and re-layouts: 237 us -> 132 us
  other arithmetic: 156 us -> 62.5 us
  Pallas kernels: 0 us -> 83.6 us
    dot_general x120 -> x24, matrix products: 536 us -> 159 us  [the longest x8 60.3 us: weight_grad(): whole = jnp.einsum('bnd,bne->de', left, right, preferred_element_type=F32)]
    reduce_scatter x4 -> x8, waiting for transfers between devices: 1020 us -> 797 us  [weight_grad(): lax.psum_scatter(whole.astype(BF16), ALL, scatter_dimension=0, tiled=True)]
    all_to_all x5 -> x1, blocking collectives: 206 us -> 52.6 us  [forward_layer(): lax.all_to_all(packed.reshape(image_count, local_rows, 3, seq_count, grou...]
    all_to_all x3 -> x1, waiting for transfers between devices: 91.8 us -> 0.01 us  [forward_layer(): lax.all_to_all(packed.reshape(image_count, local_rows, 3, seq_count, grou...]
    unnamed x14 -> x18, waiting for transfers between devices: 37.5 us -> 124 us
    pallas_call x0 -> x4, Pallas kernels: none -> 83.6 us  [the longest x2 52.3 us: attention_backward(): pl.pallas_call(functools.partial(backward_kernel, heads), grid=(count, st...]
    convert_element_type x15 -> x4, other arithmetic: 74.8 us -> 3.8 us  [per_device(): to_sections(zero, one, 0).astype(F32)[None]]
    all_to_all x1 -> x2, waiting for transfers between devices: 39.4 us -> 97.3 us  [backward_layer(): lax.all_to_all(jnp.stack(head_grads, axis=2), 'seq', split_axis=1, concat...]
  transfers between devices with their start and end apart: 22 -> 34, of which waited for: 16 -> 22; matrix products, arithmetic and copies ran while one was open for 10% -> 16% of each run, Pallas kernels for 0% -> 3%
where the time goes in v1:
time: 1800 us; the launch traced here: 1770 us
  waiting for transfers between devices  1140 us (63%)
  matrix products  159 us (9%)
  local copies, waits for them, and re-layouts  132 us (7%)
  blocking collectives  121 us (7%)
  Pallas kernels  83.6 us (5%)
  other arithmetic  62.5 us (3%)
  starting transfers between devices  49.4 us (3%)
    reduce_scatter x8, waiting for transfers between devices, weight_grad(): lax.psum_scatter(whole.astype(BF16), ALL, scatter_dimension=0, tiled=True)  797 us
    unnamed x18, waiting for transfers between devices  124 us
    all_to_all x2, waiting for transfers between devices, backward_layer(): lax.all_to_all(jnp.stack(head_grads, axis=2), 'seq', split_axis=1, concat...  97.3 us
    dot_general x8, matrix products, weight_grad(): whole = jnp.einsum('bnd,bne->de', left, right, preferred_element_type=F32)  60.3 us
    all_gather x8, waiting for transfers between devices, per_device(): lax.all_gather(pair[layer], ('dp', 'pipe'), axis=0, tiled=True)  59.1 us
    all_to_all x1, blocking collectives, forward_layer(): lax.all_to_all(packed.reshape(image_count, local_rows, 3, seq_count, grou...  52.6 us
    pallas_call x2, Pallas kernels, attention_backward(): pl.pallas_call(functools.partial(backward_kernel, heads), grid=(count, st...  52.3 us
    unnamed x1, blocking collectives  44.2 us
  transfers between devices with their start and end apart: 34, of which 22 were waited for; matrix products, arithmetic and copies ran while one was open for 16% of the time, Pallas kernels for 3%

profile of v1, /device:TPU:10, one launch (start us, length us, event | category | flops | bytes accessed | tf_op | source)
XLA Modules:
  0.0 1766.9 jit_solution(9547281946830498446)
XLA Ops:
  31.7 24.2 %all-gather.1 = f32[8,14,256]{2,1,0:T(8,128)S(1)} all-gather(f32[1,14,256]{2,1,0:T(8,128)S(1)} %maximum_bitcast_fusion), channel_id=2, replica_groups=mesh['pipe'=2,'seq'=4,'dp'=4] {'pipe','dp'}, dimensions={0}, use_global_device_ids=true | all-gather | bytes 129024 | tf_op jit(solution)/shard_map/all_gather | solution.py:307
  58.2 3.1 all-gather.11.cloned.1.call-done
  61.3 6.6 add_convert_fusion.1
  68.0 3.9 reshape.930
  73.5 5.3 all-to-all-start
  81.1 44.2 %all-reduce = s32[1376]{0:T(1024)S(1)} all-reduce(s32[1376]{0:T(1024)S(1)} %dynamic-update-slice), channel_id=1, replica_groups=mesh['pipe'=2,'seq'=4,'dp'=4] {'seq'}, use_global_device_ids=true, to_apply=%add | all-reduce | flops 1376 | bytes 11008
  125.6 15.7 shard_map.169
  141.3 8.2 copy.135
  150.0 7.3 reduce.42
  158.3 7.0 all-to-all-start.1
  166.7 13.2 all-to-all-done.1
  181.1 4.0 fusion.95
  185.9 8.5 multiply_convert_fusion.1
  194.4 10.9 all-gather.17.cloned.1.call-done
  205.3 8.4 convert_reduce_fusion.2
  214.1 39.1 %all-gather.19.cloned.1.call-done = bf16[1024,3072]{1,0:T(8,128)(2,1)} async-done(((bf16[128,3072]{1,0:T(8,128)(2,1)}), bf16[1024,3072]{1,0:T(8,128)(2,1)}) %all-gather.19.cloned.1.call-update) | async-done | bytes 6291472 | tf_op jit(solution)/shard_map/all_gather | solution.py:324
  253.2 6.7 add_convert_fusion
  259.9 3.9 reshape.935
  264.1 52.6 %all_to_all.120 = bf16[1,344,3,4,256]{4,1,2,0,3:T(8,128)(2,1)S(1)} all-to-all(bf16[1,344,3,4,256]{4,1,2,0,3:T(8,128)(2,1)S(1)} %copy.90), channel_id=1, replica_groups=mesh['pipe'=2,'seq'=4,'dp'=4] {'seq'}, dimensions={3} | all-to-all | bytes 4227072 | tf_op jit(solution)/shard_map/all_to_all | solution.py:191
  317.0 15.7 shard_map.170
  333.6 9.0 copy.134
  342.6 8.4 reduce.43
  352.0 5.4 all-to-all-start.3
  358.0 14.0 all-to-all-done.3
  376.5 3.7 fusion.93
  381.7 8.9 multiply_convert_fusion
  390.6 6.0 all-gather.25.cloned.1.call-done
  396.6 10.0 convert_reduce_fusion
  406.6 5.9 fusion.44
  413.8 7.8 convert_reduce_fusion.4
  424.9 5.3 all-to-all-start.4
  431.8 13.9 all-to-all-done.4
  456.3 26.1 %shard_map.171 = (bf16[1,1376,256]{2,1,0:T(8,128)(2,1)S(1)}, bf16[1,1376,256]{2,1,0:T(8,128)(2,1)S(1)}, bf16[1,1376,256]{2,1,0:T(8,128)(2,1)S(1)}) custom-call(bf16[1,1376,256]{2,1,0:T(8,128)(2,1)S(1)} %copy-done.14, bf16[1,1376,256]{2,1,0:T(8,128)(2,1)S(1)} %copy-done.12, bf16[1,1376,256]{2,1,0:T(8,128)(2,1)S(1)} %copy-done.10, ...), custom_call_target="tpu_custom_call" | custom-call | flops 4847042560 | bytes 4931584 | tf_op jit(solution)/shard_map/pallas_call | solution.py:160
  482.7 11.8 copy.100
  494.5 8.0 all-to-all-start.5
  505.6 56.8 %all-to-all-done.5 = bf16[1,1376,3,256]{3,2,0,1:T(4,128)(2,1)} async-done(((bf16[1,1376,3,256]{3,2,0,1:T(4,128)(2,1)}), bf16[1,1376,3,256]{3,2,0,1:T(4,128)(2,1)}, u32[]{:S(2)}, u32[]{:S(2)}) %all-to-all-start.5) | async-done | bytes 2113568 | tf_op jit(solution)/shard_map/all_to_all | solution.py:271
  562.5 5.8 copy.130
  568.3 4.8 reshape.946
  573.1 6.2 fusion.29
  582.3 8.9 convert_reduce_fusion.1
  591.2 3.9 fusion.46
  601.5 7.0 all-to-all-start.6
  608.8 14.3 all-to-all-done.6
  624.3 3.0 copy.105
  631.7 26.1 %shard_map.172 = (bf16[1,1376,256]{2,1,0:T(8,128)(2,1)S(1)}, bf16[1,1376,256]{2,1,0:T(8,128)(2,1)S(1)}, bf16[1,1376,256]{2,1,0:T(8,128)(2,1)S(1)}) custom-call(bf16[1,1376,256]{2,1,0:T(8,128)(2,1)S(1)} %copy-done.8, bf16[1,1376,256]{2,1,0:T(8,128)(2,1)S(1)} %copy-done.6, bf16[1,1376,256]{2,1,0:T(8,128)(2,1)S(1)} %copy-done.4, ...), custom_call_target="tpu_custom_call" | custom-call | flops 4847042560 | bytes 4931584 | tf_op jit(solution)/shard_map/pallas_call | solution.py:160
  658.1 11.8 copy.108
  670.0 8.0 all-to-all-start.7
  697.3 40.5 %all-to-all-done.7 = bf16[1,1376,3,256]{3,2,0,1:T(4,128)(2,1)} async-done(((bf16[1,1376,3,256]{3,2,0,1:T(4,128)(2,1)}), bf16[1,1376,3,256]{3,2,0,1:T(4,128)(2,1)}, u32[]{:S(2)}, u32[]{:S(2)}) %all-to-all-start.7) | async-done | bytes 2113568 | tf_op jit(solution)/shard_map/all_to_all | solution.py:271
  737.8 4.5 copy.129
  749.9 7.6 fusion.38
  761.6 7.3 convolution_convert_fusion.4
  769.5 8.3 convolution_convert_fusion.5
  778.5 10.4 convolution_convert_fusion.2
  789.6 10.4 convolution_convert_fusion.3
  800.7 9.9 convolution_convert_fusion
  811.7 8.7 convolution_convert_fusion.1
  820.6 3.2 select_bitcast_fusion.1
  829.8 121.2 %all-reduce.4.cloned.1.call-done = f32[32,896]{1,0:T(8,128)} async-done(((f32[32,896]{1,0:T(8,128)}), f32[32,896]{1,0:T(8,128)}) %all-reduce.4.cloned.1.call-update) | async-done | bytes 114704
  955.8 114.1 %reduce-scatter.11.cloned.1.call-done = bf16[32,3072]{1,0:T(8,128)(2,1)} async-done(((bf16[1024,3072]{1,0:T(8,128)(2,1)}), bf16[32,3072]{1,0:T(8,128)(2,1)}) %reduce-scatter.11.cloned.1.call-update) | async-done | bytes 196624 | tf_op jit(solution)/shard_map/reduce_scatter | solution.py:235
  1069.9 120.1 %reduce-scatter.9.cloned.1.call-done = bf16[32,3072]{1,0:T(8,128)(2,1)} async-done(((bf16[1024,3072]{1,0:T(8,128)(2,1)}), bf16[32,3072]{1,0:T(8,128)(2,1)}) %reduce-scatter.9.cloned.1.call-update) | async-done | bytes 196624 | tf_op jit(solution)/shard_map/reduce_scatter | solution.py:235
  1191.2 124.5 %reduce-scatter.19.cloned.1.call-done = bf16[32,4096]{1,0:T(8,128)(2,1)} async-done(((bf16[1024,4096]{1,0:T(8,128)(2,1)}), bf16[32,4096]{1,0:T(8,128)(2,1)}) %reduce-scatter.19.cloned.1.call-update) | async-done | bytes 262160 | tf_op jit(solution)/shard_map/reduce_scatter | solution.py:235
  1315.7 147.3 %reduce-scatter.17.cloned.1.call-done = bf16[32,4096]{1,0:T(8,128)(2,1)} async-done(((bf16[1024,4096]{1,0:T(8,128)(2,1)}), bf16[32,4096]{1,0:T(8,128)(2,1)}) %reduce-scatter.17.cloned.1.call-update) | async-done | bytes 262160 | tf_op jit(solution)/shard_map/reduce_scatter | solution.py:235
  1465.1 144.7 %reduce-scatter.23.cloned.1.call-done = bf16[128,1024]{1,0:T(8,128)(2,1)} async-done(((bf16[4096,1024]{1,0:T(8,128)(2,1)}), bf16[128,1024]{1,0:T(8,128)(2,1)}) %reduce-scatter.23.cloned.1.call-update) | async-done | bytes 262160 | tf_op jit(solution)/shard_map/reduce_scatter | solution.py:235
  1609.8 146.5 %reduce-scatter.21.cloned.1.call-done = bf16[128,1024]{1,0:T(8,128)(2,1)} async-done(((bf16[4096,1024]{1,0:T(8,128)(2,1)}), bf16[128,1024]{1,0:T(8,128)(2,1)}) %reduce-scatter.21.cloned.1.call-update) | async-done | bytes 262160 | tf_op jit(solution)/shard_map/reduce_scatter | solution.py:235
  (469 shorter events, 131.7 us)
Async XLA Ops:
  7.2 73.6 %copy-start = (s32[2,344]{1,0:T(2,128)S(1)}, s32[2,344]{1,0:T(2,128)}, u32[]{:S(2)}) copy-start(s32[2,344]{1,0:T(2,128)} %param.11) | copy-start | bytes 8260
  7.2 54.1 %all-gather.11.cloned.1.call-start = ((), (), s32[]{:S(2)}) async-start(), calls=%async_computation.16 | async-start | bytes 7077888 | tf_op jit(solution)/shard_map/all_gather | solution.py:324
  8.6 2.5 collective-permute-start
  13.7 167.4 %all-gather.13.cloned.1.call-start = ((), (), s32[]{:S(2)}) async-start(), calls=%async_computation.17 | async-start | bytes 2359296 | tf_op jit(solution)/shard_map/all_gather | solution.py:324
  13.8 1.6 collective-permute-start.1
  16.4 169.2 %all-gather.15.cloned.1.call-start = ((), (), s32[]{:S(2)}) async-start(), calls=%async_computation.18 | async-start | bytes 9437184 | tf_op jit(solution)/shard_map/all_gather | solution.py:324
  16.5 2.7 collective-permute-start.2
  21.0 184.3 %all-gather.17.cloned.1.call-start = ((), (), s32[]{:S(2)}) async-start(), calls=%async_computation.19 | async-start | bytes 9437184 | tf_op jit(solution)/shard_map/all_gather | solution.py:324
  23.6 2.9 collective-permute-start.3
  28.4 224.8 %all-gather.19.cloned.1.call-start = ((), (), s32[]{:S(2)}) async-start(), calls=%async_computation.20 | async-start | bytes 7077888 | tf_op jit(solution)/shard_map/all_gather | solution.py:324
  29.0 346.9 %all-gather.21.cloned.1.call-start = ((), (), s32[]{:S(2)}) async-start(), calls=%async_computation.21 | async-start | bytes 2359296 | tf_op jit(solution)/shard_map/all_gather | solution.py:324
  29.5 352.1 %all-gather.23.cloned.1.call-start = ((), (), s32[]{:S(2)}) async-start(), calls=%async_computation.22 | async-start | bytes 9437184 | tf_op jit(solution)/shard_map/all_gather | solution.py:324
  56.0 12.0 copy-start.43
  57.3 10.7 copy-start.51
  57.3 10.7 copy-start.106
  57.9 10.1 copy-start.65
  58.2 9.7 copy-start.89
  73.5 51.8 %all-to-all-start = ((bf16[1,344,3,4,256]{4,1,2,0,3:T(8,128)(2,1)}), bf16[1,344,3,4,256]{4,1,2,0,3:T(8,128)(2,1)S(1)}, u32[]{:S(2)}, u32[]{:S(2)}) async-start(bf16[1,344,3,4,256]{4,1,2,0,3:T(8,128)(2,1)} %copy.86), calls=%async_computation | async-start | bytes 4227072 | tf_op jit(solution)/shard_map/all_to_all | solution.py:191
  78.7 317.9 %all-gather.25.cloned.1.call-start = ((), (), s32[]{:S(2)}) async-start(), calls=%async_computation.23 | async-start | bytes 9437184 | tf_op jit(solution)/shard_map/all_gather | solution.py:324
  125.6 15.7 copy-start.3
  125.6 15.7 copy-start.5
  125.6 15.7 copy-start.7
  158.3 21.6 %all-to-all-start.1 = ((bf16[4,2,44032]{2,1,0:T(2,128)(2,1)}), bf16[4,2,44032]{2,1,0:T(2,128)(2,1)S(1)}, u32[]{:S(2)}, u32[]{:S(2)}) async-start(bf16[4,2,44032]{2,1,0:T(2,128)(2,1)} %reshape.993), calls=%async_computation.1 | async-start | bytes 1409024 | tf_op jit(solution)/shard_map/all_to_all | solution.py:202
  185.1 20.2 %copy-start.23 = (f32[1,344,1024]{2,1,0:T(8,128)}, f32[1,344,1024]{2,1,0:T(8,128)S(1)}, u32[]{:S(2)}) copy-start(f32[1,344,1024]{2,1,0:T(8,128)S(1)} %get-tuple-element.103) | copy-start | bytes 4227076
  185.2 9.2 copy-start.68
  185.5 8.9 copy-start.92
  213.7 39.4 %copy-start.19 = (bf16[1,344,1024]{2,1,0:T(8,128)(2,1)}, bf16[1,344,1024]{2,1,0:T(8,128)(2,1)S(1)}, u32[]{:S(2)}) copy-start(bf16[1,344,1024]{2,1,0:T(8,128)(2,1)S(1)} %get-tuple-element.101) | copy-start | bytes 2113540
  213.7 39.4 %copy-start.71 = (f32[344]{0:T(512)}, f32[344]{0:T(512)S(1)}, u32[]{:S(2)}) copy-start(f32[344]{0:T(512)S(1)} %broadcast_multiply_fusion.9) | copy-start | bytes 4132
  214.1 39.1 %copy-start.98 = (f32[344]{0:T(512)}, f32[344]{0:T(512)S(1)}, u32[]{:S(2)}) copy-start(f32[344]{0:T(512)S(1)} %add_rsqrt_fusion.1) | copy-start | bytes 4132
  317.0 15.7 copy-start.9
  317.0 15.7 copy-start.11
  317.0 15.7 copy-start.13
  352.0 20.1 %all-to-all-start.3 = ((bf16[4,2,44032]{2,1,0:T(2,128)(2,1)}), bf16[4,2,44032]{2,1,0:T(2,128)(2,1)S(1)}, u32[]{:S(2)}, u32[]{:S(2)}) async-start(bf16[4,2,44032]{2,1,0:T(2,128)(2,1)} %reshape.995), calls=%async_computation.3 | async-start | bytes 1409024 | tf_op jit(solution)/shard_map/all_to_all | solution.py:202
  380.3 32.4 %copy-start.95 = (f32[344]{0:T(512)}, f32[344]{0:T(512)S(1)}, u32[]{:S(2)}) copy-start(f32[344]{0:T(512)S(1)} %broadcast_multiply_fusion.8) | copy-start | bytes 4132
  381.6 31.1 %copy-start.119 = (f32[344]{0:T(512)}, f32[344]{0:T(512)S(1)}, u32[]{:S(2)}) copy-start(f32[344]{0:T(512)S(1)} %add_rsqrt_fusion) | copy-start | bytes 4132
  381.7 14.9 copy-start.87
  396.6 10.0 copy-start.26
  396.6 10.0 copy-start.122
  424.9 20.8 %all-to-all-start.4 = ((bf16[1,344,4,256]{3,1,0,2:T(8,128)(2,1)}), bf16[1,344,4,256]{3,1,0,2:T(8,128)(2,1)S(1)}, u32[]{:S(2)}, u32[]{:S(2)}) async-start(bf16[1,344,4,256]{3,1,0,2:T(8,128)(2,1)} %copy.96), calls=%async_computation.4 | async-start | bytes 1409024 | tf_op jit(solution)/shard_map/all_to_all | solution.py:257
  494.5 67.9 %all-to-all-start.5 = ((bf16[1,1376,3,256]{3,2,0,1:T(4,128)(2,1)}), bf16[1,1376,3,256]{3,2,0,1:T(4,128)(2,1)}, u32[]{:S(2)}, u32[]{:S(2)}) async-start(bf16[1,1376,3,256]{3,2,0,1:T(4,128)(2,1)} %copy.100), calls=%async_computation.5 | async-start | bytes 5636096 | tf_op jit(solution)/shard_map/all_to_all | solution.py:271
  502.5 322.9 %reduce-scatter.15.cloned.1.call-start = ((), (), s32[]{:S(2)}) async-start(), calls=%async_computation.27 | async-start | bytes 2162688 | tf_op jit(solution)/shard_map/reduce_scatter | solution.py:235
  580.7 10.5 slice-start
  582.2 13.6 copy-start.17
  582.3 8.9 copy-start.24
  582.3 8.9 copy-start.47
  582.3 8.9 copy-start.69
  582.3 8.9 copy-start.93
  582.3 8.9 slice-start.1
  601.5 21.6 %all-to-all-start.6 = ((bf16[1,344,4,256]{3,1,0,2:T(8,128)(2,1)}), bf16[1,344,4,256]{3,1,0,2:T(8,128)(2,1)S(1)}, u32[]{:S(2)}, u32[]{:S(2)}) async-start(bf16[1,344,4,256]{3,1,0,2:T(8,128)(2,1)} %copy.104), calls=%async_computation.6 | async-start | bytes 1409024 | tf_op jit(solution)/shard_map/all_to_all | solution.py:257
  670.0 67.8 %all-to-all-start.7 = ((bf16[1,1376,3,256]{3,2,0,1:T(4,128)(2,1)}), bf16[1,1376,3,256]{3,2,0,1:T(4,128)(2,1)}, u32[]{:S(2)}, u32[]{:S(2)}) async-start(bf16[1,1376,3,256]{3,2,0,1:T(4,128)(2,1)} %copy.108), calls=%async_computation.7 | async-start | bytes 5636096 | tf_op jit(solution)/shard_map/all_to_all | solution.py:271
  677.9 147.4 %reduce-scatter.13.cloned.1.call-start = ((), (), s32[]{:S(2)}) async-start(), calls=%async_computation.26 | async-start | bytes 2162688 | tf_op jit(solution)/shard_map/reduce_scatter | solution.py:235
  680.8 270.2 %all-reduce.4.cloned.1.call-start = ((), (), s32[]{:S(2)}) async-start(), calls=%async_computation.32 | async-start | bytes 229376
  761.1 308.8 %reduce-scatter.11.cloned.1.call-start = ((), (), s32[]{:S(2)}) async-start(), calls=%async_computation.25 | async-start | bytes 6488064 | tf_op jit(solution)/shard_map/reduce_scatter | solution.py:235
  768.9 421.2 %reduce-scatter.9.cloned.1.call-start = ((), (), s32[]{:S(2)}) async-start(), calls=%async_computation.24 | async-start | bytes 6488064 | tf_op jit(solution)/shard_map/reduce_scatter | solution.py:235
  777.8 537.8 %reduce-scatter.19.cloned.1.call-start = ((), (), s32[]{:S(2)}) async-start(), calls=%async_computation.29 | async-start | bytes 8650752 | tf_op jit(solution)/shard_map/reduce_scatter | solution.py:235
  789.0 674.0 %reduce-scatter.17.cloned.1.call-start = ((), (), s32[]{:S(2)}) async-start(), calls=%async_computation.28 | async-start | bytes 8650752 | tf_op jit(solution)/shard_map/reduce_scatter | solution.py:235
  800.0 809.8 %reduce-scatter.23.cloned.1.call-start = ((), (), s32[]{:S(2)}) async-start(), calls=%async_computation.31 | async-start | bytes 8650752 | tf_op jit(solution)/shard_map/reduce_scatter | solution.py:235
  810.7 945.7 %reduce-scatter.21.cloned.1.call-start = ((), (), s32[]{:S(2)}) async-start(), calls=%async_computation.30 | async-start | bytes 8650752 | tf_op jit(solution)/shard_map/reduce_scatter | solution.py:235
  823.8 2.6 collective-permute-start.4
  824.8 129.7 %collective-permute-start.5 = (bf16[1,344,1024]{2,1,0:T(8,128)(2,1)S(1)}, bf16[1,344,1024]{2,1,0:T(8,128)(2,1)S(1)}, u32[]{:S(2)}, u32[]{:S(2)}) collective-permute-start(bf16[1,344,1024]{2,1,0:T(8,128)(2,1)S(1)} %broadcast_select_fusion), channel_id=1, source_target_pairs={{0,16},{16,0},{1,17},{17,1},{2,18},{18,2},{3,19},{19,3},{4,20},{20... | collective-permute-start | bytes 2113544 | tf_op jit(solution)/shard_map/ppermute | solution.py:50
  826.2 2.8 collective-permute-start.7
  1191.1 273.1 %collective-permute-start.6 = (bf16[32,3072]{1,0:T(8,128)(2,1)S(1)}, bf16[32,3072]{1,0:T(8,128)(2,1)S(1)}, u32[]{:S(2)}, u32[]{:S(2)}) collective-permute-start(bf16[32,3072]{1,0:T(8,128)(2,1)S(1)} %get-tuple-element.129), channel_id=1, source_target_pairs={{0,16},{16,0},{1,17},{17,1},{2,18},{18,2},{3,19},{19,3},{4,20},{20... | collective-permute-start | bytes 589832 | tf_op jit(solution)/shard_map/ppermute | solution.py:50
  1464.1 293.4 %collective-permute-start.8 = (bf16[32,4096]{1,0:T(8,128)(2,1)S(1)}, bf16[32,4096]{1,0:T(8,128)(2,1)S(1)}, u32[]{:S(2)}, u32[]{:S(2)}) collective-permute-start(bf16[32,4096]{1,0:T(8,128)(2,1)S(1)} %get-tuple-element.127), channel_id=1, source_target_pairs={{0,16},{16,0},{1,17},{17,1},{2,18},{18,2},{3,19},{19,3},{4,20},{20... | collective-permute-start | bytes 786440 | tf_op jit(solution)/shard_map/ppermute | solution.py:50
  1757.4 1.6 collective-permute-start.9
  (103 other events, 334.1 us)
Sparse Core Ops, SparseCore 0:
  13.8 47.4 all-gather.10
  63.2 28.4 all-gather.12
  94.1 54.3 all-gather.14
  150.9 54.3 all-gather.16
  207.6 45.5 all-gather.18
  255.5 27.8 all-gather.20
  285.9 54.3 all-gather.22
  342.2 54.3 all-gather.24
  505.8 132.7 reduce-scatter.14
  680.9 130.6 reduce-scatter.12
  817.8 133.1 all-reduce.3
  956.5 113.3 reduce-scatter.10
  1076.5 113.5 reduce-scatter.8
  1192.2 123.4 reduce-scatter.18
  1317.8 145.1 reduce-scatter.16
  1465.2 144.6 reduce-scatter.22
  1612.0 144.3 reduce-scatter.20

commit v2 on v1

--- a/solution.py
+++ b/solution.py
@@ -14,7 +14,7 @@
 epsilon = 1e-06
 root_half = 0.7071067811865476
 inv_root_tau = 0.3989422804014327
-ALL = ("seq", "dp", "pipe")
+SHARDS = ("seq", "dp")
 F32 = jnp.float32
 BF16 = jnp.bfloat16
 
@@ -215,12 +215,13 @@
     return (output, kept)
 
 
-def backward_layer(kept, cotangent, hidden_keys, weight_set):
+def backward_layer(kept, cotangent, hidden_keys, weight_set, early, late):
     w_qkv, w_proj, w_fc1, w_fc2, gains, biases, fc1_bias = weight_set
     (
         normed_one, factor_one, normed_in, head_sets, merged, log_total, token_outs,
         branch_one, normed_two, factor_two, second, hidden, active, branch_two,
     ) = kept
+    core = lax.axis_index("pipe")
     seq_count = lax.axis_size("seq")
     group_width = D // seq_count
     image_count, local_rows = cotangent.shape[:2]
@@ -231,8 +232,12 @@
         return jnp.sum(values, axis=token_axes, dtype=F32)
 
     def weight_grad(left, right):
-        whole = jnp.einsum("bnd,bne->de", left, right, preferred_element_type=F32)
-        return lax.psum_scatter(whole.astype(BF16), ALL, scatter_dimension=0, tiled=True)
+        whole = jnp.einsum("bnd,bne->de", left, right, preferred_element_type=F32).astype(BF16)
+        half = whole.shape[1] // 2
+        mine = lax.dynamic_slice_in_dim(whole, core * half, half, axis=1)
+        theirs = swap(lax.dynamic_slice_in_dim(whole, (1 - core) * half, half, axis=1))
+        both = (mine.astype(F32) + theirs.astype(F32)).astype(BF16)
+        return lax.psum_scatter(both, SHARDS, scatter_dimension=0, tiled=True)
 
     upstream = cotangent.astype(F32)
     grad_branch = (gains[3] * upstream).astype(BF16)
@@ -261,6 +266,7 @@
         concat_axis=1,
         tiled=True,
     ).reshape(image_count, full_rows, group_width)
+    head_upward, early = lax.optimization_barrier((head_upward, early))
     delta = jnp.sum(
         (head_upward.astype(F32) * merged.astype(F32)).reshape(image_count, full_rows, -1, HD),
         axis=-1,
@@ -271,6 +277,7 @@
     grad_packed = lax.all_to_all(
         jnp.stack(head_grads, axis=2), "seq", split_axis=1, concat_axis=3, tiled=True
     ).reshape(image_count, local_rows, 3 * D)
+    grad_packed, grad_down, late = lax.optimization_barrier((grad_packed, grad_down, late))
     grad_inproj = weight_grad(normed_in, grad_packed)
     grad_bias_query = total(grad_packed[..., :D])
     grad_bias_value = total(grad_packed[..., 2 * D :])
@@ -289,6 +296,8 @@
         grad_frames.astype(BF16),
         (grad_inproj, grad_outproj, grad_upper, grad_down),
         (rows, grad_bias_mid),
+        early,
+        late,
     )
 
 
@@ -305,7 +314,7 @@
     part = gains.shape[2]
     small = jnp.concatenate([gains[0], biases[0], fc1_bias[0].reshape(-1, part)], axis=0)
     small = lax.all_gather(small, ("pipe", "dp"), axis=0)
-    visible = lax.all_gather(my_images(key_mask), "seq", axis=1, tiled=True) > 0
+    visible = my_images(lax.all_gather(key_mask, "seq", axis=1, tiled=True)) > 0
     hidden_keys = jnp.where(visible, 0.0, -1e30).astype(F32)
 
     halves = []
@@ -328,25 +337,28 @@
     middle, kept_zero = forward_layer(my_images(images), hidden_keys, sets[0])
     final, kept_one = forward_layer(middle, hidden_keys, sets[1])
     section_outputs = to_sections(middle, final, 0)[None]
-    grad_middle, weights_one, vectors_one = backward_layer(
-        kept_one, my_images(out_grad), hidden_keys, sets[1]
-    )
-    grad_first, weights_zero, vectors_zero = backward_layer(
-        kept_zero, grad_middle, hidden_keys, sets[0]
-    )
+    grad_middle, weights_one, vectors_one, _, _ = backward_layer(
+        kept_one, my_images(out_grad), hidden_keys, sets[1], (), ()
+    )
+    inproj_one, outproj_one, upper_one, down_one = weights_one
+    grad_first, weights_zero, vectors_zero, (upper_one,), (inproj_one, outproj_one) = backward_layer(
+        kept_zero, grad_middle, hidden_keys, sets[0], (upper_one,), (inproj_one, outproj_one)
+    )
+    weights_one = (inproj_one, outproj_one, upper_one, down_one)
     input_grads = to_sections(grad_first, grad_middle, 0)[None]
 
     packed = []
     for rows, mids in (vectors_zero, vectors_one):
         lines = rows.reshape(10, shards, -1).transpose(1, 0, 2).reshape(shards, -1)
         packed.append(jnp.concatenate([lines, mids.reshape(shards, -1)], axis=1))
+    both = jnp.where(low, packed[0], packed[1]) + swap(jnp.where(low, packed[1], packed[0]))
     mine = lax.psum_scatter(
-        jnp.concatenate(packed, axis=0), ("pipe", "seq", "dp"), scatter_dimension=0, tiled=True
-    )[0]
+        both.reshape(shards * 8, -1), SHARDS, scatter_dimension=0, tiled=True
+    ).reshape(-1)
     width = D // shards
     lines = mine[: 10 * width].reshape(10, width)
     weights = [
-        to_sections(zero, one, 0).astype(F32)[None]
+        to_sections(zero, one, 1).astype(F32)[None]
         for zero, one in zip(weights_zero, weights_one)
     ]
     return (

time: 1800 us -> 1320 us (0.73); the launches traced: 1770 us -> 1310 us
  waiting for transfers between devices: 1140 us -> 472 us
  blocking collectives: 121 us -> 282 us
  other arithmetic: 62.5 us -> 104 us
  local copies, waits for them, and re-layouts: 132 us -> 160 us
    reduce_scatter x8, waiting for transfers between devices: 797 us -> 275 us  [weight_grad(): return lax.psum_scatter(both, SHARDS, scatter_dimension=0, tiled=True)]
    unnamed x18 -> x16, waiting for transfers between devices: 124 us -> 1.95 us
    all_to_all x0 -> x1, blocking collectives: none -> 78.7 us  [backward_layer(): lax.all_to_all(jnp.stack(head_grads, axis=2), 'seq', split_axis=1, concat...]
    all_gather x0 -> x1, blocking collectives: none -> 52.8 us  [per_device(): visible = my_images(lax.all_gather(key_mask, 'seq', axis=1, tiled=True)) > 0]
    all_to_all x2 -> x1, waiting for transfers between devices: 97.3 us -> 57.7 us  [backward_layer(): lax.all_to_all(jnp.stack(head_grads, axis=2), 'seq', split_axis=1, concat...]
    convert_element_type x4 -> x12, other arithmetic: 3.8 us -> 40.8 us  [the longest x8 35 us: weight_grad(): both = (mine.astype(F32) + theirs.astype(F32)).astype(BF16)]
    unnamed x1, blocking collectives: 44.2 us -> 73.4 us
    ppermute x10 -> x19, waiting for transfers between devices: 9.51 us -> 34.2 us  [swap(): return lax.ppermute(block, 'pipe', [(0, 1), (1, 0)])]
  transfers between devices with their start and end apart: 34 -> 41, of which waited for: 22 -> 21; matrix products, arithmetic and copies ran while one was open for 16% -> 30% of each run, Pallas kernels for 3% -> 6%
where the time goes in v2:
time: 1320 us; the launch traced here: 1310 us
  waiting for transfers between devices  472 us (36%)
  blocking collectives  282 us (21%)
  local copies, waits for them, and re-layouts  160 us (12%)
  matrix products  146 us (11%)
  other arithmetic  104 us (8%)
  Pallas kernels  83.6 us (6%)
  starting transfers between devices  42.1 us (3%)
  between operations  16.1 us (1%)
    reduce_scatter x8, waiting for transfers between devices, weight_grad(): return lax.psum_scatter(both, SHARDS, scatter_dimension=0, tiled=True)  275 us
    all_to_all x1, blocking collectives, backward_layer(): lax.all_to_all(jnp.stack(head_grads, axis=2), 'seq', split_axis=1, concat...  78.7 us
    unnamed x1, blocking collectives  73.4 us
    all_to_all x1, waiting for transfers between devices, backward_layer(): lax.all_to_all(jnp.stack(head_grads, axis=2), 'seq', split_axis=1, concat...  57.7 us
    all_gather x1, blocking collectives, per_device(): visible = my_images(lax.all_gather(key_mask, 'seq', axis=1, tiled=True)) > 0  52.8 us
    all_to_all x1, blocking collectives, forward_layer(): lax.all_to_all(packed.reshape(image_count, local_rows, 3, seq_count, grou...  52.6 us
    pallas_call x2, Pallas kernels, attention_backward(): pl.pallas_call(functools.partial(backward_kernel, heads), grid=(count, st...  52.3 us
    all_gather x8, waiting for transfers between devices, per_device(): lax.all_gather(pair[layer], ('dp', 'pipe'), axis=0, tiled=True)  46.4 us
  transfers between devices with their start and end apart: 41, of which 21 were waited for; matrix products, arithmetic and copies ran while one was open for 30% of the time, Pallas kernels for 6%

profile of v2, /device:TPU:10, one launch (start us, length us, event | category | flops | bytes accessed | tf_op | source)
XLA Modules:
  0.0 1306.1 jit_solution(3519381034039101359)
XLA Ops:
  32.4 24.3 %all-gather.1 = f32[8,14,256]{2,1,0:T(8,128)S(1)} all-gather(f32[1,14,256]{2,1,0:T(8,128)S(1)} %maximum_bitcast_fusion), channel_id=2, replica_groups=mesh['pipe'=2,'seq'=4,'dp'=4] {'pipe','dp'}, dimensions={0}, use_global_device_ids=true | all-gather | bytes 129024 | tf_op jit(solution)/shard_map/all_gather | solution.py:316
  60.2 6.7 add_convert_fusion.7
  66.9 3.9 reshape.904
  72.4 5.3 all-to-all-start
  77.7 52.8 %all-gather.2 = s32[4,344,2]{1,2,0:T(2,128)S(1)} all-gather(s32[1,344,2]{1,2,0:T(2,128)S(1)} %bitcast.423), channel_id=1, replica_groups=mesh['pipe'=2,'seq'=4,'dp'=4] {'seq'}, dimensions={0}, use_global_device_ids=true | all-gather | bytes 13760 | tf_op jit(solution)/shard_map/all_gather | solution.py:317
  131.5 15.7 %shard_map.169 = (bf16[1,1376,256]{2,1,0:T(8,128)(2,1)S(1)}, f32[1,1376,4]{2,1,0:T(8,128)S(1)}) custom-call(bf16[1,1376,256]{2,1,0:T(8,128)(2,1)S(1)} %get-tuple-element.97.q_ref, bf16[1,1376,256]{2,1,0:T(8,128)(2,1)S(1)} %get-tuple-element.96.k_ref, bf16[1,1376,256]{2,1,0:T(8,128)(2,1)S(1)} %get-tuple-element.95.v_ref, ...), custom_call_target="tpu_custom_call" | custom-call | flops 1938817024 | bytes 2818048 | tf_op jit(solution)/shard_map/pallas_call | solution.py:95
  148.1 8.1 copy.133
  156.7 7.3 reduce.34
  165.0 5.0 all-to-all-start.1
  171.2 12.0 all-to-all-done.1
  189.9 8.4 multiply_convert_fusion.1
  198.3 6.1 all-gather.18.cloned.1.call-done
  204.4 8.5 convert_reduce_fusion.2
  213.2 39.0 %all-gather.20.cloned.1.call-done = bf16[1024,3072]{1,0:T(8,128)(2,1)} async-done(((bf16[128,3072]{1,0:T(8,128)(2,1)}), bf16[1024,3072]{1,0:T(8,128)(2,1)}) %all-gather.20.cloned.1.call-update) | async-done | bytes 6291472 | tf_op jit(solution)/shard_map/all_gather | solution.py:333
  252.3 6.6 add_convert_fusion.6
  258.9 4.9 reshape.909
  265.7 52.6 %all_to_all.120 = bf16[1,344,3,4,256]{4,1,2,0,3:T(8,128)(2,1)S(1)} all-to-all(bf16[1,344,3,4,256]{4,1,2,0,3:T(8,128)(2,1)S(1)} %copy.89), channel_id=1, replica_groups=mesh['pipe'=2,'seq'=4,'dp'=4] {'seq'}, dimensions={3} | all-to-all | bytes 4227072 | tf_op jit(solution)/shard_map/all_to_all | solution.py:191
  318.6 15.7 %shard_map.170 = (bf16[1,1376,256]{2,1,0:T(8,128)(2,1)S(1)}, f32[1,1376,4]{2,1,0:T(8,128)S(1)}) custom-call(bf16[1,1376,256]{2,1,0:T(8,128)(2,1)S(1)} %get-tuple-element.94.q_ref, bf16[1,1376,256]{2,1,0:T(8,128)(2,1)S(1)} %get-tuple-element.93.k_ref, bf16[1,1376,256]{2,1,0:T(8,128)(2,1)S(1)} %get-tuple-element.92.v_ref, ...), custom_call_target="tpu_custom_call" | custom-call | flops 1938817024 | bytes 2818048 | tf_op jit(solution)/shard_map/pallas_call | solution.py:95
  334.3 9.0 copy.132
  343.4 8.4 reduce.35
  352.7 5.0 all-to-all-start.3
  358.5 13.8 %all-to-all-done.3 = bf16[4,2,44032]{2,1,0:T(2,128)(2,1)S(1)} async-done(((bf16[4,2,44032]{2,1,0:T(2,128)(2,1)}), bf16[4,2,44032]{2,1,0:T(2,128)(2,1)S(1)}, u32[]{:S(2)}, u32[]{:S(2)}) %all-to-all-start.3) | async-done | bytes 704544 | tf_op jit(solution)/shard_map/all_to_all | solution.py:202
  382.1 8.6 multiply_convert_fusion
  390.7 4.9 convolution_convert_fusion.3
  396.2 7.1 collective-permute-done.5
  403.4 3.9 add_convert_fusion.3
  407.4 8.8 convert_reduce_fusion
  416.2 5.5 convolution_convert_fusion.2
  426.4 8.6 fusion.50
  436.9 7.9 add_convert_fusion.2
  445.5 11.0 convert_reduce_fusion.4
  459.7 6.7 all-to-all-start.4
  467.0 15.4 %all-to-all-done.4 = bf16[1,344,4,256]{3,1,0,2:T(8,128)(2,1)S(1)} async-done(((bf16[1,344,4,256]{3,1,0,2:T(8,128)(2,1)}), bf16[1,344,4,256]{3,1,0,2:T(8,128)(2,1)S(1)}, u32[]{:S(2)}, u32[]{:S(2)}) %all-to-all-start.4) | async-done | bytes 704544 | tf_op jit(solution)/shard_map/all_to_all | solution.py:262
  492.0 26.1 %shard_map.171 = (bf16[1,1376,256]{2,1,0:T(8,128)(2,1)S(1)}, bf16[1,1376,256]{2,1,0:T(8,128)(2,1)S(1)}, bf16[1,1376,256]{2,1,0:T(8,128)(2,1)S(1)}) custom-call(bf16[1,1376,256]{2,1,0:T(8,128)(2,1)S(1)} %copy-done.13, bf16[1,1376,256]{2,1,0:T(8,128)(2,1)S(1)} %copy-done.11, bf16[1,1376,256]{2,1,0:T(8,128)(2,1)S(1)} %copy-done.9, ...), custom_call_target="tpu_custom_call" | custom-call | flops 4847042560 | bytes 4931584 | tf_op jit(solution)/shard_map/pallas_call | solution.py:160
  518.4 11.8 copy.99
  530.2 8.0 all-to-all-start.5
  541.0 57.7 %all-to-all-done.5 = bf16[1,1376,3,256]{3,2,0,1:T(4,128)(2,1)} async-done(((bf16[1,1376,3,256]{3,2,0,1:T(4,128)(2,1)}), bf16[1,1376,3,256]{3,2,0,1:T(4,128)(2,1)}, u32[]{:S(2)}, u32[]{:S(2)}) %all-to-all-start.5) | async-done | bytes 2113568 | tf_op jit(solution)/shard_map/all_to_all | solution.py:277
  598.8 5.9 copy.128
  604.6 4.8 reshape.920
  609.4 5.7 convolution_convert_fusion.5
  620.5 5.9 collective-permute-done.9
  629.7 6.8 fusion.35
  639.5 5.6 add_convert_fusion.5
  645.2 6.7 convolution_convert_fusion.1
  652.6 7.1 collective-permute-done.7
  663.8 8.7 convert_reduce_fusion.1
  672.5 5.3 convolution_convert_fusion
  678.5 7.3 fusion.52
  689.0 4.0 add_convert_fusion
  697.0 6.9 all-to-all-start.6
  704.3 15.5 %all-to-all-done.6 = bf16[1,344,4,256]{3,1,0,2:T(8,128)(2,1)S(1)} async-done(((bf16[1,344,4,256]{3,1,0,2:T(8,128)(2,1)}), bf16[1,344,4,256]{3,1,0,2:T(8,128)(2,1)S(1)}, u32[]{:S(2)}, u32[]{:S(2)}) %all-to-all-start.6) | async-done | bytes 704544 | tf_op jit(solution)/shard_map/all_to_all | solution.py:262
  728.5 26.1 %shard_map.172 = (bf16[1,1376,256]{2,1,0:T(8,128)(2,1)S(1)}, bf16[1,1376,256]{2,1,0:T(8,128)(2,1)S(1)}, bf16[1,1376,256]{2,1,0:T(8,128)(2,1)S(1)}) custom-call(bf16[1,1376,256]{2,1,0:T(8,128)(2,1)S(1)} %copy-done.7, bf16[1,1376,256]{2,1,0:T(8,128)(2,1)S(1)} %copy-done.5, bf16[1,1376,256]{2,1,0:T(8,128)(2,1)S(1)} %copy-done.3, ...), custom_call_target="tpu_custom_call" | custom-call | flops 4847042560 | bytes 4931584 | tf_op jit(solution)/shard_map/pallas_call | solution.py:160
  754.9 10.8 copy.107
  765.7 78.7 %all_to_all.121 = bf16[1,1376,3,256]{3,2,0,1:T(4,128)(2,1)S(1)} all-to-all(bf16[1,1376,3,256]{3,2,0,1:T(4,128)(2,1)S(1)} %copy.107), channel_id=1, replica_groups=mesh['pipe'=2,'seq'=4,'dp'=4] {'seq'}, dimensions={1} | all-to-all | bytes 4227072 | tf_op jit(solution)/shard_map/all_to_all | solution.py:277
  849.9 38.4 %reduce-scatter.15.cloned.1.call-done = bf16[64,1536]{1,0:T(8,128)(2,1)} async-done(((bf16[1024,1536]{1,0:T(8,128)(2,1)}), bf16[64,1536]{1,0:T(8,128)(2,1)}) %reduce-scatter.15.cloned.1.call-update) | async-done | bytes 196624 | tf_op jit(solution)/shard_map/reduce_scatter | solution.py:240
  888.3 96.9 %reduce-scatter.13.cloned.1.call-done = bf16[256,512]{1,0:T(8,128)(2,1)} async-done(((bf16[4096,512]{1,0:T(8,128)(2,1)}), bf16[256,512]{1,0:T(8,128)(2,1)}) %reduce-scatter.13.cloned.1.call-update) | async-done | bytes 262160 | tf_op jit(solution)/shard_map/reduce_scatter | solution.py:240
  985.3 5.6 convolution_convert_fusion.4
  995.7 5.1 collective-permute-done.13
  1002.5 5.5 add_convert_fusion.4
  1041.9 40.3 %reduce-scatter.23.cloned.1.call-done = bf16[64,2048]{1,0:T(8,128)(2,1)} async-done(((bf16[1024,2048]{1,0:T(8,128)(2,1)}), bf16[64,2048]{1,0:T(8,128)(2,1)}) %reduce-scatter.23.cloned.1.call-update) | async-done | bytes 262160 | tf_op jit(solution)/shard_map/reduce_scatter | solution.py:240
  1084.1 7.2 fusion.44
  1108.0 44.1 %reduce-scatter.21.cloned.1.call-done = bf16[64,512]{1,0:T(8,128)(2,1)} async-done(((bf16[1024,512]{1,0:T(8,128)(2,1)}), bf16[64,512]{1,0:T(8,128)(2,1)}) %reduce-scatter.21.cloned.1.call-update) | async-done | bytes 65552 | tf_op jit(solution)/shard_map/reduce_scatter | solution.py:240
  1160.3 73.4 %all-reduce = f32[128,112]{1,0:T(8,128)S(1)} all-reduce(f32[128,112]{1,0:T(8,128)S(1)} %reshape.935), channel_id=11, replica_groups=mesh['pipe'=2,'seq'=4,'dp'=4] {'seq','dp'}, use_global_device_ids=true, to_apply=%region_48.49.clone | all-reduce | flops 14336 | bytes 114688
  1239.4 55.5 %reduce-scatter.19.cloned.1.call-done = bf16[64,1536]{1,0:T(8,128)(2,1)} async-done(((bf16[1024,1536]{1,0:T(8,128)(2,1)}), bf16[64,1536]{1,0:T(8,128)(2,1)}) %reduce-scatter.19.cloned.1.call-update) | async-done | bytes 196624 | tf_op jit(solution)/shard_map/reduce_scatter | solution.py:240
  (461 shorter events, 194.9 us)
Async XLA Ops:
  7.2 53.0 %all-gather.12.cloned.1.call-start = ((), (), s32[]{:S(2)}) async-start(), calls=%async_computation.16 | async-start | bytes 7077888 | tf_op jit(solution)/shard_map/all_gather | solution.py:333
  8.5 2.4 collective-permute-start
  12.4 172.8 %all-gather.14.cloned.1.call-start = ((), (), s32[]{:S(2)}) async-start(), calls=%async_computation.17 | async-start | bytes 2359296 | tf_op jit(solution)/shard_map/all_gather | solution.py:333
  13.6 1.6 collective-permute-start.1
  17.1 172.4 %all-gather.16.cloned.1.call-start = ((), (), s32[]{:S(2)}) async-start(), calls=%async_computation.18 | async-start | bytes 9437184 | tf_op jit(solution)/shard_map/all_gather | solution.py:333
  17.3 2.7 collective-permute-start.2
  21.8 182.6 %all-gather.18.cloned.1.call-start = ((), (), s32[]{:S(2)}) async-start(), calls=%async_computation.19 | async-start | bytes 9437184 | tf_op jit(solution)/shard_map/all_gather | solution.py:333
  24.3 2.9 collective-permute-start.3
  29.1 223.2 %all-gather.20.cloned.1.call-start = ((), (), s32[]{:S(2)}) async-start(), calls=%async_computation.20 | async-start | bytes 7077888 | tf_op jit(solution)/shard_map/all_gather | solution.py:333
  29.7 346.6 %all-gather.22.cloned.1.call-start = ((), (), s32[]{:S(2)}) async-start(), calls=%async_computation.21 | async-start | bytes 2359296 | tf_op jit(solution)/shard_map/all_gather | solution.py:333
  30.3 351.8 %all-gather.24.cloned.1.call-start = ((), (), s32[]{:S(2)}) async-start(), calls=%async_computation.22 | async-start | bytes 9437184 | tf_op jit(solution)/shard_map/all_gather | solution.py:333
  58.0 131.5 %copy-start.57 = (f32[1,4,256]{2,0,1:T(1,128)}, f32[1,4,256]{2,0,1:T(1,128)S(1)}, u32[]{:S(2)}) copy-start(f32[1,4,256]{2,0,1:T(1,128)S(1)} %get-tuple-element.129) | copy-start | bytes 12292
  72.4 58.8 %all-to-all-start = ((bf16[1,344,3,4,256]{4,1,2,0,3:T(8,128)(2,1)}), bf16[1,344,3,4,256]{4,1,2,0,3:T(8,128)(2,1)S(1)}, u32[]{:S(2)}, u32[]{:S(2)}) async-start(bf16[1,344,3,4,256]{4,1,2,0,3:T(8,128)(2,1)} %copy.84), calls=%async_computation | async-start | bytes 4227072 | tf_op jit(solution)/shard_map/all_to_all | solution.py:191
  165.0 18.2 %all-to-all-start.1 = ((bf16[4,2,44032]{2,1,0:T(2,128)(2,1)}), bf16[4,2,44032]{2,1,0:T(2,128)(2,1)S(1)}, u32[]{:S(2)}, u32[]{:S(2)}) async-start(bf16[4,2,44032]{2,1,0:T(2,128)(2,1)} %reshape.961), calls=%async_computation.1 | async-start | bytes 1409024 | tf_op jit(solution)/shard_map/all_to_all | solution.py:202
  170.0 237.3 %all-gather.26.cloned.1.call-start = ((), (), s32[]{:S(2)}) async-start(), calls=%async_computation.23 | async-start | bytes 9437184 | tf_op jit(solution)/shard_map/all_gather | solution.py:333
  204.4 47.9 %copy-start.78 = (f32[3072]{0:T(1024)S(1)}, f32[3072]{0:T(1024)}, u32[]{:S(2)}) copy-start(f32[3072]{0:T(1024)} %get-tuple-element.140) | copy-start | bytes 36868
  204.4 47.9 %copy-start.92 = (f32[1,4,256]{2,0,1:T(1,128)S(1)}, f32[1,4,256]{2,0,1:T(1,128)}, u32[]{:S(2)}) copy-start(f32[1,4,256]{2,0,1:T(1,128)} %get-tuple-element.123) | copy-start | bytes 12292
  212.9 46.0 %copy-start.18 = (bf16[1,344,1024]{2,1,0:T(8,128)(2,1)}, bf16[1,344,1024]{2,1,0:T(8,128)(2,1)S(1)}, u32[]{:S(2)}) copy-start(bf16[1,344,1024]{2,1,0:T(8,128)(2,1)S(1)} %get-tuple-element.81) | copy-start | bytes 2113540
  213.2 45.7 %copy-start.83 = (f32[344]{0:T(512)}, f32[344]{0:T(512)S(1)}, u32[]{:S(2)}) copy-start(f32[344]{0:T(512)S(1)} %add_rsqrt_fusion.1) | copy-start | bytes 4132
  318.6 15.7 %copy-start.8 = (bf16[1,1376,256]{2,1,0:T(8,128)(2,1)}, bf16[1,1376,256]{2,1,0:T(8,128)(2,1)S(1)}, u32[]{:S(2)}) copy-start(bf16[1,1376,256]{2,1,0:T(8,128)(2,1)S(1)} %get-tuple-element.92.v_ref) | copy-start | bytes 2113540
  318.6 15.7 %copy-start.10 = (bf16[1,1376,256]{2,1,0:T(8,128)(2,1)}, bf16[1,1376,256]{2,1,0:T(8,128)(2,1)S(1)}, u32[]{:S(2)}) copy-start(bf16[1,1376,256]{2,1,0:T(8,128)(2,1)S(1)} %get-tuple-element.93.k_ref) | copy-start | bytes 2113540
  318.6 15.7 %copy-start.12 = (bf16[1,1376,256]{2,1,0:T(8,128)(2,1)}, bf16[1,1376,256]{2,1,0:T(8,128)(2,1)S(1)}, u32[]{:S(2)}) copy-start(bf16[1,1376,256]{2,1,0:T(8,128)(2,1)S(1)} %get-tuple-element.94.q_ref) | copy-start | bytes 2113540
  352.7 19.6 %all-to-all-start.3 = ((bf16[4,2,44032]{2,1,0:T(2,128)(2,1)}), bf16[4,2,44032]{2,1,0:T(2,128)(2,1)S(1)}, u32[]{:S(2)}, u32[]{:S(2)}) async-start(bf16[4,2,44032]{2,1,0:T(2,128)(2,1)} %reshape.963), calls=%async_computation.3 | async-start | bytes 1409024 | tf_op jit(solution)/shard_map/all_to_all | solution.py:202
  357.7 251.7 %reduce-scatter.9.cloned.1.call-start = ((), (), s32[]{:S(2)}) async-start(), calls=%async_computation.24 | async-start | bytes 4456448 | tf_op jit(solution)/shard_map/reduce_scatter | solution.py:240
  396.1 7.2 collective-permute-start.5
  407.3 297.1 %reduce-scatter.11.cloned.1.call-start = ((), (), s32[]{:S(2)}) async-start(), calls=%async_computation.25 | async-start | bytes 4456448 | tf_op jit(solution)/shard_map/reduce_scatter | solution.py:240
  426.4 10.6 collective-permute-start.6
  459.7 22.7 %all-to-all-start.4 = ((bf16[1,344,4,256]{3,1,0,2:T(8,128)(2,1)}), bf16[1,344,4,256]{3,1,0,2:T(8,128)(2,1)S(1)}, u32[]{:S(2)}, u32[]{:S(2)}) async-start(bf16[1,344,4,256]{3,1,0,2:T(8,128)(2,1)} %copy.95), calls=%async_computation.4 | async-start | bytes 1409024 | tf_op jit(solution)/shard_map/all_to_all | solution.py:262
  530.2 68.5 %all-to-all-start.5 = ((bf16[1,1376,3,256]{3,2,0,1:T(4,128)(2,1)}), bf16[1,1376,3,256]{3,2,0,1:T(4,128)(2,1)}, u32[]{:S(2)}, u32[]{:S(2)}) async-start(bf16[1,1376,3,256]{3,2,0,1:T(4,128)(2,1)} %copy.99), calls=%async_computation.5 | async-start | bytes 5636096 | tf_op jit(solution)/shard_map/all_to_all | solution.py:277
  538.2 311.8 %reduce-scatter.17.cloned.1.call-start = ((), (), s32[]{:S(2)}) async-start(), calls=%async_computation.28 | async-start | bytes 1114112 | tf_op jit(solution)/shard_map/reduce_scatter | solution.py:240
  618.9 20.6 %collective-permute-start.8 = (bf16[1024,1536]{1,0:T(8,128)(2,1)}, bf16[1024,1536]{1,0:T(8,128)(2,1)}, u32[]{:S(2)}, u32[]{:S(2)}) collective-permute-start(bf16[1024,1536]{1,0:T(8,128)(2,1)} %constant_dynamic-slice_fusion.4), channel_id=1, source_target_pairs={{0,16},{16,0},{1,17},{17,1},{2,18},{18,2},{3,19},{19,3},{4,20},{20... | collective-permute-start | bytes 9437192 | tf_op jit(solution)/shard_map/ppermute | solution.py:50
  620.0 6.4 collective-permute-start.9
  629.2 259.1 %reduce-scatter.15.cloned.1.call-start = ((), (), s32[]{:S(2)}) async-start(), calls=%async_computation.27 | async-start | bytes 3342336 | tf_op jit(solution)/shard_map/reduce_scatter | solution.py:240
  639.5 47.1 %copy-start.15 = (bf16[1,344,1024]{2,1,0:T(8,128)(2,1)}, bf16[1,344,1024]{2,1,0:T(8,128)(2,1)S(1)}, u32[]{:S(2)}) copy-start(bf16[1,344,1024]{2,1,0:T(8,128)(2,1)S(1)} %get-tuple-element.72) | copy-start | bytes 2113540
  645.1 340.1 %reduce-scatter.13.cloned.1.call-start = ((), (), s32[]{:S(2)}) async-start(), calls=%async_computation.26 | async-start | bytes 4456448 | tf_op jit(solution)/shard_map/reduce_scatter | solution.py:240
  652.4 7.2 collective-permute-start.7
  663.5 418.7 %reduce-scatter.23.cloned.1.call-start = ((), (), s32[]{:S(2)}) async-start(), calls=%async_computation.31 | async-start | bytes 4456448 | tf_op jit(solution)/shard_map/reduce_scatter | solution.py:240
  678.4 10.6 collective-permute-start.15
  697.0 22.9 %copy-start.1 = (bf16[1,1376,256]{2,1,0:T(8,128)(2,1)S(1)}, bf16[1,1376,256]{2,1,0:T(8,128)(2,1)}, u32[]{:S(2)}) copy-start(bf16[1,1376,256]{2,1,0:T(8,128)(2,1)} %copy-done) | copy-start | bytes 2113540
  697.0 22.9 %all-to-all-start.6 = ((bf16[1,344,4,256]{3,1,0,2:T(8,128)(2,1)}), bf16[1,344,4,256]{3,1,0,2:T(8,128)(2,1)S(1)}, u32[]{:S(2)}, u32[]{:S(2)}) async-start(bf16[1,344,4,256]{3,1,0,2:T(8,128)(2,1)} %copy.103), calls=%async_computation.7 | async-start | bytes 1409024 | tf_op jit(solution)/shard_map/all_to_all | solution.py:262
  703.9 448.2 %reduce-scatter.21.cloned.1.call-start = ((), (), s32[]{:S(2)}) async-start(), calls=%async_computation.30 | async-start | bytes 1114112 | tf_op jit(solution)/shard_map/reduce_scatter | solution.py:240
  847.1 138.2 %copy-start.34 = (bf16[2,344,1024]{2,1,0:T(8,128)(2,1)S(1)}, bf16[2,344,1024]{2,1,0:T(8,128)(2,1)}, u32[]{:S(2)}) copy-start(bf16[2,344,1024]{2,1,0:T(8,128)(2,1)} %param.10) | copy-start | bytes 4227076
  847.1 138.2 %copy-start.60 = (f32[1,4,256]{2,0,1:T(1,128)S(1)}, f32[1,4,256]{2,0,1:T(1,128)}, u32[]{:S(2)}) copy-start(f32[1,4,256]{2,0,1:T(1,128)} %copy-done.59) | copy-start | bytes 12292
  847.1 138.2 %copy-start.65 = (f32[344]{0:T(512)S(1)}, f32[344]{0:T(512)}, u32[]{:S(2)}) copy-start(f32[344]{0:T(512)} %copy-done.64) | copy-start | bytes 4132
  847.1 138.2 %copy-start.80 = (f32[344]{0:T(512)S(1)}, f32[344]{0:T(512)}, u32[]{:S(2)}) copy-start(f32[344]{0:T(512)} %copy-done.79) | copy-start | bytes 4132
  847.1 138.1 %copy-start.87 = (f32[1,4,256]{2,0,1:T(1,128)S(1)}, f32[1,4,256]{2,0,1:T(1,128)}, u32[]{:S(2)}) copy-start(f32[1,4,256]{2,0,1:T(1,128)} %copy-done.86) | copy-start | bytes 12292
  993.7 8.8 collective-permute-start.11
  995.1 5.7 collective-permute-start.13
  1002.3 292.7 %reduce-scatter.19.cloned.1.call-start = ((), (), s32[]{:S(2)}) async-start(), calls=%async_computation.29 | async-start | bytes 3342336 | tf_op jit(solution)/shard_map/reduce_scatter | solution.py:240
  1011.2 6.8 collective-permute-start.4
  1036.3 47.8 %copy-start.25 = (bf16[1,344,3072]{2,1,0:T(8,128)(2,1)S(1)}, bf16[1,344,3072]{2,1,0:T(8,128)(2,1)}, u32[]{:S(2)}) copy-start(bf16[1,344,3072]{2,1,0:T(8,128)(2,1)} %reshape.929) | copy-start | bytes 6340612
  1084.1 153.2 %collective-permute-start.16 = (bf16[64,2048]{1,0:T(8,128)(2,1)}, bf16[64,2048]{1,0:T(8,128)(2,1)}, u32[]{:S(2)}, u32[]{:S(2)}) collective-permute-start(bf16[64,2048]{1,0:T(8,128)(2,1)} %get-tuple-element.107), channel_id=1, source_target_pairs={{0,16},{16,0},{1,17},{17,1},{2,18},{18,2},{3,19},{19,3},{4,20},{20... | collective-permute-start | bytes 786440 | tf_op jit(solution)/shard_map/ppermute | solution.py:50
  1094.2 60.8 %copy-start.16 = (bf16[1,344,1024]{2,1,0:T(8,128)(2,1)S(1)}, bf16[1,344,1024]{2,1,0:T(8,128)(2,1)}, u32[]{:S(2)}) copy-start(bf16[1,344,1024]{2,1,0:T(8,128)(2,1)} %copy-done.15) | copy-start | bytes 2113540
  1094.2 60.8 %copy-start.31 = (f32[344,1024]{1,0:T(8,128)S(1)}, f32[344,1024]{1,0:T(8,128)}, u32[]{:S(2)}) copy-start(f32[344,1024]{1,0:T(8,128)} %get-tuple-element.153) | copy-start | bytes 4227076
  1094.2 60.8 %copy-start.66 = (f32[344]{0:T(512)S(1)}, f32[344]{0:T(512)}, u32[]{:S(2)}) copy-start(f32[344]{0:T(512)} %copy-done.64) | copy-start | bytes 4132
  1108.0 51.4 %collective-permute-start.18 = (f32[16,896]{1,0:T(8,128)}, f32[16,896]{1,0:T(8,128)}, u32[]{:S(2)}, u32[]{:S(2)}) collective-permute-start(f32[16,896]{1,0:T(8,128)} %broadcast_select_fusion.6), channel_id=1, source_target_pairs={{0,16},{16,0},{1,17},{17,1},{2,18},{18,2},{3,19},{19,3},{4,20},{20... | collective-permute-start | bytes 172040 | tf_op jit(solution)/shard_map/ppermute | solution.py:50
  1153.6 82.0 %collective-permute-start.14 = (bf16[64,512]{1,0:T(8,128)(2,1)}, bf16[64,512]{1,0:T(8,128)(2,1)}, u32[]{:S(2)}, u32[]{:S(2)}) collective-permute-start(bf16[64,512]{1,0:T(8,128)(2,1)} %get-tuple-element.111), channel_id=1, source_target_pairs={{0,16},{16,0},{1,17},{17,1},{2,18},{18,2},{3,19},{19,3},{4,20},{20... | collective-permute-start | bytes 196616 | tf_op jit(solution)/shard_map/ppermute | solution.py:50
  1157.6 78.0 %copy-start.55 = (bf16[1,64,512]{2,1,0:T(8,128)(2,1)S(1)}, bf16[1,64,512]{2,1,0:T(8,128)(2,1)}, u32[]{:S(2)}) copy-start(bf16[1,64,512]{2,1,0:T(8,128)(2,1)} %get-tuple-element.110) | copy-start | bytes 196612
  1158.7 78.6 %copy-start.45 = (bf16[1,64,2048]{2,1,0:T(8,128)(2,1)S(1)}, bf16[1,64,2048]{2,1,0:T(8,128)(2,1)}, u32[]{:S(2)}) copy-start(bf16[1,64,2048]{2,1,0:T(8,128)(2,1)} %get-tuple-element.106) | copy-start | bytes 786436
  1158.7 136.2 %copy-start.56 = (bf16[64,1536]{1,0:T(8,128)(2,1)S(1)}, bf16[64,1536]{1,0:T(8,128)(2,1)}, u32[]{:S(2)}) copy-start(bf16[64,1536]{1,0:T(8,128)(2,1)} %reduce-scatter.15.cloned.1.call-done) | copy-start | bytes 589828
  1158.7 137.2 %collective-permute-start.17 = (bf16[256,512]{1,0:T(8,128)(2,1)S(1)}, bf16[256,512]{1,0:T(8,128)(2,1)S(1)}, u32[]{:S(2)}, u32[]{:S(2)}) collective-permute-start(bf16[256,512]{1,0:T(8,128)(2,1)S(1)} %get-tuple-element.105), channel_id=1, source_target_pairs={{0,16},{16,0},{1,17},{17,1},{2,18},{18,2},{3,19},{19,3},{4,20},{20... | collective-permute-start | bytes 786440 | tf_op jit(solution)/shard_map/ppermute | solution.py:50
  1159.3 137.8 %collective-permute-start.10 = (bf16[1,344,1024]{2,1,0:T(8,128)(2,1)S(1)}, bf16[1,344,1024]{2,1,0:T(8,128)(2,1)S(1)}, u32[]{:S(2)}, u32[]{:S(2)}) collective-permute-start(bf16[1,344,1024]{2,1,0:T(8,128)(2,1)S(1)} %broadcast_select_fusion), channel_id=1, source_target_pairs={{0,16},{16,0},{1,17},{17,1},{2,18},{18,2},{3,19},{19,3},{4,20},{20... | collective-permute-start | bytes 2113544 | tf_op jit(solution)/shard_map/ppermute | solution.py:50
  1239.4 57.7 %copy-start.35 = (bf16[1,1,344,1024]{3,2,1,0:T(8,128)(2,1)S(1)}, bf16[1,1,344,1024]{3,2,1,0:T(8,128)(2,1)}, u32[]{:S(2)}) copy-start(bf16[1,1,344,1024]{3,2,1,0:T(8,128)(2,1)} %get-tuple-element.76) | copy-start | bytes 2113540
  1295.9 2.5 collective-permute-start.12
  (89 other events, 479.7 us)
Sparse Core Ops, SparseCore 0:
  12.6 47.6 all-gather.11
  62.1 28.5 all-gather.13
  93.2 54.3 all-gather.15
  150.0 54.3 all-gather.17
  206.7 45.5 all-gather.19
  254.6 27.8 all-gather.21
  285.0 54.3 all-gather.23
  341.3 54.3 all-gather.25
  407.4 98.5 reduce-scatter.8
  508.1 128.0 reduce-scatter.10
  639.0 96.2 reduce-scatter.16
  740.9 147.3 reduce-scatter.14
  890.7 94.4 reduce-scatter.12
  987.5 94.7 reduce-scatter.22
  1085.0 67.0 reduce-scatter.20
  1156.9 137.9 reduce-scatter.18
